TPU v7x, 256 devices: a whole 4x4x8 slice. The times are simulated.
256 devices in a mesh: row: 16 (over y, x), col: 16 (over z, core).
Axes of the slice: x: 4, y: 4, z: 8, core: 2. Of those that a mesh axis runs over, the one named last changes fastest.
Arguments:
- matrix: float32 [8, 16, 128, 8, 16, 128], P(None, 'row', None, None, 'col'), as said below
Outputs:
- updated: float32 [8, 16, 128, 8, 16, 128], P(None, 'row', None, None, 'col')
- images: float32 [8, 8, 16, 128], P(None, None, 'row')
Inputs may be any that keep to these rules, and one draw needn't show every extreme that they name: The matrix is symmetric: entry (r, c) equals entry (c, r).
All inputs are finite; a program needn't handle non-finite values.
Results may differ from a plain program's by a relative error of at most 0.00016.
Values sent between devices are 32-bit elements; how exact they have to be, the bound alone decides.
No kernel may reach another device: no remote copies, remote signals or barrier semaphores. Data moves between devices by JAX's collectives and lax.ppermute only.
A program may use at most 128 MiB of HBM per device.

v0:
```python
import functools

import jax
import jax.numpy as jnp
from jax import lax
from jax.sharding import Mesh
from jax.sharding import PartitionSpec as P

K = 8
ROW = ("row_0", "row_1")


epsilon = 1e-06
highest = lax.Precision.HIGHEST


def from_root(value, axis, root):
    return lax.dynamic_index_in_dim(lax.all_gather(value, axis), root, 0, keepdims=False)


def by_axis(value, axes):
    return functools.reduce(lax.psum, axes, value)


def from_everyone(value, axis):
    copies = jnp.broadcast_to(value, (lax.axis_size(axis), *value.shape))
    return lax.all_to_all(copies, axis, split_axis=0, concat_axis=0, tiled=True)


def over_copies(value, axis):
    everything = from_everyone(value, axis)
    return jnp.sum(everything, axis=0)


def in_one(arrays, axis):
    vector, at, finished = (jnp.concatenate([a.reshape(-1) for a in arrays]), 0, [])
    running = over_copies(vector, axis)
    for a in arrays:
        finished.append(running[at : at + a.size].reshape(a.shape))
        at += a.size
    return tuple(finished)


def product(left_side, right_side):
    return jnp.dot(left_side, right_side, precision=highest)


def body(matrix):
    row_blocks = matrix.shape[0]
    block_size = matrix.shape[2]
    col_blocks = matrix.shape[3]
    row_total = row_blocks * block_size
    col_total = col_blocks * block_size
    tile = matrix.reshape(row_total, col_total)
    row_count = lax.axis_size(ROW)
    col_count = lax.axis_size("col")
    row_index = lax.axis_index(ROW)
    col_index = lax.axis_index("col")
    row_ids = (
        (jnp.arange(row_blocks, dtype=jnp.int32)[:, None] * row_count + row_index) * block_size
        + jnp.arange(block_size, dtype=jnp.int32)[None, :]
    ).reshape(-1)
    col_ids = (
        (jnp.arange(col_blocks, dtype=jnp.int32)[:, None] * col_count + col_index) * block_size
        + jnp.arange(block_size, dtype=jnp.int32)[None, :]
    ).reshape(-1)
    owner = row_index == 0
    panel = from_root(tile[:, :K], "col", 0)
    reflectors = jnp.zeros((row_total, K), jnp.float32)
    images_mat = jnp.zeros((row_total, K), jnp.float32)
    refl_cols = jnp.zeros((col_total, K), jnp.float32)
    images_cols = jnp.zeros((col_total, K), jnp.float32)
    panel_top = from_root(tile[:K, :], ROW, 0)
    col_parts = []
    for position in range(K):
        if position > 0:
            head_pair = jnp.where(
                owner, jnp.stack([reflectors[position], images_mat[position]]), 0.0
            )
            head_pair = by_axis(head_pair, ROW)
            column = (
                panel[:, position]
                - product(reflectors, head_pair[1])
                - product(images_mat, head_pair[0])
            )
            column_c = (
                panel_top[position]
                - product(refl_cols, head_pair[1])
                - product(images_cols, head_pair[0])
            )
        else:
            column = panel[:, 0]
            column_c = panel_top[0]
        below_diag = jnp.where(row_ids > position, column, 0.0)
        first_part = jnp.where(owner, column[position + 1], 0.0)
        square_sum, first_entry = (
            by_axis(jnp.sum(below_diag * below_diag), ROW),
            by_axis(first_part, ROW),
        )
        col_norm = jnp.sqrt(square_sum)
        denom = jnp.sqrt(2.0 * col_norm * (col_norm + first_entry) + epsilon)
        vector = below_diag + jnp.where(row_ids == position + 1, col_norm, 0.0)
        reflector = vector / denom
        below_c = jnp.where(col_ids > position, column_c, 0.0)
        in_columns = (below_c + jnp.where(col_ids == position + 1, col_norm, 0.0)) / denom
        partial_value = product(tile, in_columns)
        image_vec = over_copies(partial_value, "col")
        image_c = by_axis(product(reflector, tile), ROW)
        proj_w = product(images_mat.T, reflector)
        proj_v = product(reflectors.T, reflector)
        sum_w, sum_v = in_one((proj_w, proj_v), ROW)
        image_vec = image_vec - product(reflectors, sum_w) - product(images_mat, sum_v)
        gamma_val = by_axis(product(reflector, image_vec), ROW)
        update = 2.0 * image_vec - 2.0 * gamma_val * reflector
        image_c = image_c - product(refl_cols, sum_w) - product(images_cols, sum_v)
        update_c = 2.0 * image_c - 2.0 * gamma_val * in_columns
        refl_cols = refl_cols.at[:, position].set(in_columns)
        images_cols = images_cols.at[:, position].set(update_c)
        reflectors = reflectors.at[:, position].set(reflector)
        images_mat = images_mat.at[:, position].set(update)
        col_parts.append(in_columns)
    left_side = jnp.concatenate([reflectors, images_mat], axis=1)
    right_side = jnp.concatenate([images_cols, refl_cols], axis=1)
    updated = tile - product(left_side, right_side.T)
    return (updated.reshape(matrix.shape), images_mat.T.reshape(K, row_blocks, 1, block_size))


def solution(mesh):
    torus = Mesh(mesh.devices.reshape(4, 4, mesh.shape["col"]), ("row_0", "row_1", "col"))
    in_specs = (P(None, ROW, None, None, "col", None),)
    out_specs = (P(None, ROW, None, None, "col", None), P(None, None, ROW, None))
    return jax.shard_map(body, mesh=torus, in_specs=in_specs, out_specs=out_specs, check_vma=False)
```

profile of v0, /device:TPU:1, one launch (start us, length us, event | category | flops | bytes accessed | tf_op | source)
XLA Modules:
  0.0 940.5 jit_solution(6204862638050453319)
XLA Ops:
  3.9 59.0 %all-gather = f32[16384,8]{1,0:T(8,128)S(1)} all-gather(f32[1024,8]{1,0:T(8,128)S(1)} %slice.860), channel_id=2, replica_groups=mesh['row_0'=4,'row_1'=4,'col'=16] {'col'}, dimensions={0}, use_global_device_ids=true | all-gather | bytes 557056 | tf_op jit(solution)/shard_map/all_gather | solution.py:18
  67.6 9.4 all-reduce.21
  77.0 9.1 all-reduce.12
  94.2 19.5 %all-gather.1 = f32[128,1024]{1,0:T(8,128)S(1)} all-gather(f32[8,1024]{1,0:T(8,128)S(1)} %slice.864), channel_id=3, replica_groups=mesh['row_0'=4,'row_1'=4,'col'=16] {'row_0','row_1'}, dimensions={0}, use_global_device_ids=true | all-gather | bytes 557056 | tf_op jit(solution)/shard_map/all_gather | solution.py:18
  129.9 13.0 %all-to-all-start = ((f32[16,1,1024]{2,1,0:T(1,128)}), f32[16,1,1024]{2,1,0:T(1,128)S(1)}, u32[]{:S(2)}, u32[]{:S(2)}) async-start(f32[16,1,1024]{2,1,0:T(1,128)} %broadcast_in_dim.142), calls=%async_computation | async-start | bytes 131072 | tf_op jit(solution)/shard_map/all_to_all | solution.py:27
  152.8 9.1 psum.550
  161.9 7.2 psum.551
  170.6 7.2 psum.552
  177.7 6.2 psum.553
  187.1 7.7 all-reduce.20
  194.7 7.5 all-reduce.11
  232.2 16.2 %all-to-all-start.2 = ((f32[16,1,1024]{2,1,0:T(1,128)}), f32[16,1,1024]{2,1,0:T(1,128)S(1)}, u32[]{:S(2)}, u32[]{:S(2)}) async-start(f32[16,1,1024]{2,1,0:T(1,128)} %broadcast_in_dim.146), calls=%async_computation.2 | async-start | bytes 131072 | tf_op jit(solution)/shard_map/all_to_all | solution.py:27
  249.6 6.6 all-to-all-done.2
  258.5 9.4 %psum.560 = f32[]{:T(128)} all-reduce(f32[]{:T(128)} %multiply_reduce_fusion.6), channel_id=1, replica_groups=mesh['row_0'=4,'row_1'=4,'col'=16] {'row_0'}, use_global_device_ids=true, to_apply=%region_23.24 | all-reduce | flops 1 | bytes 8 | tf_op jit(solution)/shard_map/psum | solution.py:22
  269.5 9.0 psum.561
  282.5 6.0 psum.562
  288.5 6.0 psum.563
  297.6 8.2 all-reduce.19
  305.8 8.6 all-reduce.10
  325.9 5.9 fusion.294
  344.3 16.2 %all-to-all-start.4 = ((f32[16,1,1024]{2,1,0:T(1,128)}), f32[16,1,1024]{2,1,0:T(1,128)S(1)}, u32[]{:S(2)}, u32[]{:S(2)}) async-start(f32[16,1,1024]{2,1,0:T(1,128)} %broadcast_in_dim.149), calls=%async_computation.4 | async-start | bytes 131072 | tf_op jit(solution)/shard_map/all_to_all | solution.py:27
  368.9 7.5 psum.570
  378.7 7.9 psum.571
  390.7 6.9 psum.572
  397.6 6.6 psum.573
  407.2 7.5 all-reduce.18
  414.6 7.7 all-reduce.9
  433.9 5.9 fusion.292
  452.2 17.1 %all-to-all-start.6 = ((f32[16,1,1024]{2,1,0:T(1,128)}), f32[16,1,1024]{2,1,0:T(1,128)S(1)}, u32[]{:S(2)}, u32[]{:S(2)}) async-start(f32[16,1,1024]{2,1,0:T(1,128)} %broadcast_in_dim.152), calls=%async_computation.6 | async-start | bytes 131072 | tf_op jit(solution)/shard_map/all_to_all | solution.py:27
  477.8 7.5 psum.580
  487.5 7.5 psum.581
  499.2 6.9 psum.582
  506.1 6.6 psum.583
  515.7 7.4 all-reduce.17
  523.1 7.7 all-reduce.8
  542.4 5.9 fusion.290
  560.8 17.2 %all-to-all-start.8 = ((f32[16,1,1024]{2,1,0:T(1,128)}), f32[16,1,1024]{2,1,0:T(1,128)S(1)}, u32[]{:S(2)}, u32[]{:S(2)}) async-start(f32[16,1,1024]{2,1,0:T(1,128)} %broadcast_in_dim.155), calls=%async_computation.8 | async-start | bytes 131072 | tf_op jit(solution)/shard_map/all_to_all | solution.py:27
  586.4 7.5 psum.590
  596.2 7.9 psum.591
  608.2 6.9 psum.592
  615.1 6.6 psum.593
  624.7 7.4 all-reduce.16
  632.1 7.7 all-reduce.7
  651.5 5.9 fusion.288
  669.8 17.4 %all-to-all-start.10 = ((f32[16,1,1024]{2,1,0:T(1,128)}), f32[16,1,1024]{2,1,0:T(1,128)S(1)}, u32[]{:S(2)}, u32[]{:S(2)}) async-start(f32[16,1,1024]{2,1,0:T(1,128)} %broadcast_in_dim.158), calls=%async_computation.10 | async-start | bytes 131072 | tf_op jit(solution)/shard_map/all_to_all | solution.py:27
  695.6 7.5 psum.600
  705.3 7.5 psum.601
  716.9 6.9 psum.602
  723.8 6.6 psum.603
  733.4 7.4 all-reduce.15
  740.9 7.7 all-reduce.6
  760.1 5.9 fusion.286
  778.4 17.3 %all-to-all-start.12 = ((f32[16,1,1024]{2,1,0:T(1,128)}), f32[16,1,1024]{2,1,0:T(1,128)S(1)}, u32[]{:S(2)}, u32[]{:S(2)}) async-start(f32[16,1,1024]{2,1,0:T(1,128)} %broadcast_in_dim.161), calls=%async_computation.12 | async-start | bytes 131072 | tf_op jit(solution)/shard_map/all_to_all | solution.py:27
  804.2 7.5 psum.610
  813.9 7.7 psum.611
  825.9 6.9 psum.612
  832.7 6.6 psum.613
  842.3 7.4 all-reduce.14
  849.8 7.7 all-reduce.5
  873.3 5.9 fusion.284
  880.4 16.4 %all-to-all-start.14 = ((f32[16,1,1024]{2,1,0:T(1,128)}), f32[16,1,1024]{2,1,0:T(1,128)S(1)}, u32[]{:S(2)}, u32[]{:S(2)}) async-start(f32[16,1,1024]{2,1,0:T(1,128)} %broadcast_in_dim.164), calls=%async_computation.14 | async-start | bytes 131072 | tf_op jit(solution)/shard_map/all_to_all | solution.py:27
  905.1 9.5 %all-reduce.13 = (f32[]{:T(128)}, f32[1024]{0:T(1024)S(1)}) all-reduce(f32[]{:T(128)} %multiply_reduce_fusion, f32[1024]{0:T(1024)S(1)} %bitcast.927), channel_id=1, replica_groups=mesh['row_0'=4,'row_1'=4,'col'=16] {'row_0'}, use_global_device_ids=true, to_apply=%region_105.106 | all-reduce | flops 1025 | bytes 8200 | tf_op jit(solution)/shard_map/psum | solution.py:22
  914.6 9.1 all-reduce.4
  930.7 6.3 subtract_bitcast_fusion
  (348 shorter events, 311.4 us)
Async XLA Ops:
  3.8 59.1 %copy-start.4 = (f32[128,8,8,128]{3,1,2,0:T(8,128)}, f32[128,8,8,128]{3,1,2,0:T(8,128)S(1)}, u32[]{:S(2)}) copy-start(f32[128,8,8,128]{3,1,2,0:T(8,128)S(1)} %copy.232) | copy-start | bytes 12582916
  62.9 3.2 copy-start.1
  88.4 40.8 %all-to-all-start.1 = ((f32[16,1,16]{2,1,0:T(1,128)}), f32[16,1,16]{2,1,0:T(1,128)S(1)}, u32[]{:S(2)}, u32[]{:S(2)}) async-start(f32[16,1,16]{2,1,0:T(1,128)} %broadcast_in_dim.143), calls=%async_computation.1 | async-start | bytes 16384 | tf_op jit(solution)/shard_map/all_to_all | solution.py:27
  114.1 5.6 copy-start
  129.1 80.7 %copy-start.2 = (f32[1024,1]{1,0:T(8,128)}, f32[1024,1]{1,0:T(8,128)S(1)}, u32[]{:S(2)}) copy-start(f32[1024,1]{1,0:T(8,128)S(1)} %divide_select_fusion) | copy-start | bytes 12292
  129.9 20.8 %all-to-all-start = ((f32[16,1,1024]{2,1,0:T(1,128)}), f32[16,1,1024]{2,1,0:T(1,128)S(1)}, u32[]{:S(2)}, u32[]{:S(2)}) async-start(f32[16,1,1024]{2,1,0:T(1,128)} %broadcast_in_dim.142), calls=%async_computation | async-start | bytes 131072 | tf_op jit(solution)/shard_map/all_to_all | solution.py:27
  211.2 20.4 %all-to-all-start.3 = ((f32[16,1,16]{2,1,0:T(1,128)}), f32[16,1,16]{2,1,0:T(1,128)S(1)}, u32[]{:S(2)}, u32[]{:S(2)}) async-start(f32[16,1,16]{2,1,0:T(1,128)} %broadcast_in_dim.147), calls=%async_computation.3 | async-start | bytes 16384 | tf_op jit(solution)/shard_map/all_to_all | solution.py:27
  215.5 7.3 copy-start.3
  232.2 24.0 %all-to-all-start.2 = ((f32[16,1,1024]{2,1,0:T(1,128)}), f32[16,1,1024]{2,1,0:T(1,128)S(1)}, u32[]{:S(2)}, u32[]{:S(2)}) async-start(f32[16,1,1024]{2,1,0:T(1,128)} %broadcast_in_dim.146), calls=%async_computation.2 | async-start | bytes 131072 | tf_op jit(solution)/shard_map/all_to_all | solution.py:27
  333.8 9.8 %all-to-all-start.5 = ((f32[16,1,16]{2,1,0:T(1,128)}), f32[16,1,16]{2,1,0:T(1,128)S(1)}, u32[]{:S(2)}, u32[]{:S(2)}) async-start(f32[16,1,16]{2,1,0:T(1,128)} %broadcast_in_dim.150), calls=%async_computation.5 | async-start | bytes 16384 | tf_op jit(solution)/shard_map/all_to_all | solution.py:27
  344.3 24.0 %all-to-all-start.4 = ((f32[16,1,1024]{2,1,0:T(1,128)}), f32[16,1,1024]{2,1,0:T(1,128)S(1)}, u32[]{:S(2)}, u32[]{:S(2)}) async-start(f32[16,1,1024]{2,1,0:T(1,128)} %broadcast_in_dim.149), calls=%async_computation.4 | async-start | bytes 131072 | tf_op jit(solution)/shard_map/all_to_all | solution.py:27
  441.8 9.8 %all-to-all-start.7 = ((f32[16,1,16]{2,1,0:T(1,128)}), f32[16,1,16]{2,1,0:T(1,128)S(1)}, u32[]{:S(2)}, u32[]{:S(2)}) async-start(f32[16,1,16]{2,1,0:T(1,128)} %broadcast_in_dim.153), calls=%async_computation.7 | async-start | bytes 16384 | tf_op jit(solution)/shard_map/all_to_all | solution.py:27
  452.2 24.9 %all-to-all-start.6 = ((f32[16,1,1024]{2,1,0:T(1,128)}), f32[16,1,1024]{2,1,0:T(1,128)S(1)}, u32[]{:S(2)}, u32[]{:S(2)}) async-start(f32[16,1,1024]{2,1,0:T(1,128)} %broadcast_in_dim.152), calls=%async_computation.6 | async-start | bytes 131072 | tf_op jit(solution)/shard_map/all_to_all | solution.py:27
  550.3 9.8 %all-to-all-start.9 = ((f32[16,1,16]{2,1,0:T(1,128)}), f32[16,1,16]{2,1,0:T(1,128)S(1)}, u32[]{:S(2)}, u32[]{:S(2)}) async-start(f32[16,1,16]{2,1,0:T(1,128)} %broadcast_in_dim.156), calls=%async_computation.9 | async-start | bytes 16384 | tf_op jit(solution)/shard_map/all_to_all | solution.py:27
  560.8 25.0 %all-to-all-start.8 = ((f32[16,1,1024]{2,1,0:T(1,128)}), f32[16,1,1024]{2,1,0:T(1,128)S(1)}, u32[]{:S(2)}, u32[]{:S(2)}) async-start(f32[16,1,1024]{2,1,0:T(1,128)} %broadcast_in_dim.155), calls=%async_computation.8 | async-start | bytes 131072 | tf_op jit(solution)/shard_map/all_to_all | solution.py:27
  659.4 9.8 %all-to-all-start.11 = ((f32[16,1,16]{2,1,0:T(1,128)}), f32[16,1,16]{2,1,0:T(1,128)S(1)}, u32[]{:S(2)}, u32[]{:S(2)}) async-start(f32[16,1,16]{2,1,0:T(1,128)} %broadcast_in_dim.159), calls=%async_computation.11 | async-start | bytes 16384 | tf_op jit(solution)/shard_map/all_to_all | solution.py:27
  669.8 25.1 %all-to-all-start.10 = ((f32[16,1,1024]{2,1,0:T(1,128)}), f32[16,1,1024]{2,1,0:T(1,128)S(1)}, u32[]{:S(2)}, u32[]{:S(2)}) async-start(f32[16,1,1024]{2,1,0:T(1,128)} %broadcast_in_dim.158), calls=%async_computation.10 | async-start | bytes 131072 | tf_op jit(solution)/shard_map/all_to_all | solution.py:27
  768.0 9.8 %all-to-all-start.13 = ((f32[16,1,16]{2,1,0:T(1,128)}), f32[16,1,16]{2,1,0:T(1,128)S(1)}, u32[]{:S(2)}, u32[]{:S(2)}) async-start(f32[16,1,16]{2,1,0:T(1,128)} %broadcast_in_dim.162), calls=%async_computation.13 | async-start | bytes 16384 | tf_op jit(solution)/shard_map/all_to_all | solution.py:27
  778.4 25.1 %all-to-all-start.12 = ((f32[16,1,1024]{2,1,0:T(1,128)}), f32[16,1,1024]{2,1,0:T(1,128)S(1)}, u32[]{:S(2)}, u32[]{:S(2)}) async-start(f32[16,1,1024]{2,1,0:T(1,128)} %broadcast_in_dim.161), calls=%async_computation.12 | async-start | bytes 131072 | tf_op jit(solution)/shard_map/all_to_all | solution.py:27
  865.7 14.1 %all-to-all-start.15 = ((f32[16,1,16]{2,1,0:T(1,128)}), f32[16,1,16]{2,1,0:T(1,128)S(1)}, u32[]{:S(2)}, u32[]{:S(2)}) async-start(f32[16,1,16]{2,1,0:T(1,128)} %broadcast_in_dim.165), calls=%async_computation.15 | async-start | bytes 16384 | tf_op jit(solution)/shard_map/all_to_all | solution.py:27
  880.4 24.0 %all-to-all-start.14 = ((f32[16,1,1024]{2,1,0:T(1,128)}), f32[16,1,1024]{2,1,0:T(1,128)S(1)}, u32[]{:S(2)}, u32[]{:S(2)}) async-start(f32[16,1,1024]{2,1,0:T(1,128)} %broadcast_in_dim.164), calls=%async_computation.14 | async-start | bytes 131072 | tf_op jit(solution)/shard_map/all_to_all | solution.py:27
where the time goes:
time: 955 us; the launch traced here: 941 us
  blocking collectives  426 us (45%)
  starting transfers between devices  159 us (17%)
  matrix products  129 us (14%)
  local copies, waits for them, and re-layouts  109 us (11%)
  other arithmetic  50.3 us (5%)
  waiting for transfers between devices  43.5 us (5%)
  between operations  23.6 us (2%)
    psum x46, blocking collectives, by_axis(): return functools.reduce(lax.psum, axes, value)  348 us
    all_to_all x16, starting transfers between devices, from_everyone(): return lax.all_to_all(copies, axis, split_axis=0, concat_axis=0, tiled=True)  159 us
    dot_general x88, matrix products, product(): return jnp.dot(left_side, right_side, precision=highest)  129 us
    all_gather x2, blocking collectives, from_root(): lax.all_gather(value, axis)  78.5 us
    all_to_all x16, waiting for transfers between devices, from_everyone(): return lax.all_to_all(copies, axis, split_axis=0, concat_axis=0, tiled=True)  43.5 us
    another operation x34, other arithmetic  31 us
  transfers between devices with their start and end apart: 16, of which 13 were waited for; matrix products, arithmetic and copies ran while one was open for 10% of the time, Pallas kernels for 0%

commit v1 on v0

v1 whole, which is shorter than its diff:
```python
import functools

import jax
import jax.numpy as jnp
from jax import lax
from jax.experimental import pallas as pl
from jax.experimental.pallas import tpu as pltpu
from jax.sharding import PartitionSpec as P

K = 8
EPS = 1e-06
PEERS = 16
F32 = jnp.float32
SCOPED = 16 * 1024 * 1024


def vmem():
    return pl.BlockSpec(memory_space=pltpu.VMEM)


def smem():
    return pl.BlockSpec(memory_space=pltpu.SMEM)


def head(slab, entry):
    return jnp.broadcast_to(slab[0:1, entry : entry + 1], slab.shape)


def total(slab):
    by_lane = jnp.sum(slab, axis=0, keepdims=True)
    return jnp.broadcast_to(jnp.sum(by_lane, axis=1, keepdims=True), slab.shape)


def dot(left, right):
    return total(jnp.sum(left * right, axis=0))


def slab_index(shape, axis):
    return lax.broadcasted_iota(jnp.int32, shape, axis)


def full_ids():
    shape = (PEERS, 8, 128)
    first = (slab_index(shape, 0) == 0) & (slab_index(shape, 1) == 0)
    return jnp.where(first, slab_index(shape, 2), 1024)


def own_ids(mine):
    shape = (8, 128)
    first = (slab_index(shape, 0) == 0) & (mine == 0)
    return jnp.where(first, slab_index(shape, 1), 1024)


def times_cols(tile, x, out):
    def rows(a, carry):
        start = pl.multiple_of(a * 128, 128)
        acc = tile[0, pl.ds(start, 128), :] * x[0:1, :]
        for b in range(1, 8):
            acc += tile[b, pl.ds(start, 128), :] * x[b : b + 1, :]
        out[pl.ds(a, 1), :] = jnp.sum(acc.T, axis=0, keepdims=True)
        return carry

    lax.fori_loop(0, 8, rows, 0)


def times_rows(tile, x_ref, out):
    def rows(a, sums):
        start = pl.multiple_of(a * 128, 128)
        x = jnp.broadcast_to(x_ref[pl.ds(a, 1), :], (128, 128)).T
        return tuple(
            s + jnp.sum((tile[b, pl.ds(start, 128), :] * x).reshape(16, 8, 128), axis=0)
            for b, s in enumerate(sums)
        )

    sums = lax.fori_loop(0, 8, rows, (jnp.zeros((8, 128), F32),) * 8)
    for b in range(8):
        out[b : b + 1, :] = jnp.sum(sums[b], axis=0, keepdims=True)


def send(payload, slabs):
    for n, slab in enumerate(slabs):
        for q in range(PEERS):
            payload[q, n] = slab


def first_kernel(place, panel, tile, payload, product):
    x = jnp.where(own_ids(place[1]) > 0, panel[0], 0.0)
    times_cols(tile, x, product)
    send(payload, [product[...], panel[0], panel[1]])


def finish_image(j, got, us, ws, coeffs):
    y = got
    for k in range(j):
        y = y - us[k][...] * coeffs[k] - ws[k][...] * coeffs[K + k]
    gamma = dot(us[j][...], y)
    return y, gamma, 2.0 * y - 2.0 * gamma * us[j][...]


def step_kernel(j, *refs):
    refs = list(refs)
    place, got, panel = refs[:3]
    del refs[:3]
    late = refs.pop(0) if j % 2 else got
    tile = refs.pop(0) if j < K - 1 else None
    us = [refs.pop(0) for _ in range(j)]
    ws = [refs.pop(0) for _ in range(max(j - 1, 0))]
    coeffs_before = refs.pop(0) if j > 0 else None
    payload, u_out, coeffs = refs[:3]
    del refs[:3]
    if j > 0:
        w_out = refs.pop(0)
    y_ref, x_ref, product = refs
    mine = place[j % 2]
    ids = full_ids()
    summed = got[0, 0]
    for q in range(1, PEERS):
        summed = summed + got[q, 0]
    at = {0: 1, 1: 2}.get(j, 3 if j % 2 else 2)
    column, column_own = late[:, at], late[mine, at]
    next_own = panel[j + 1] if j % 2 else late[mine, at + 1]
    x = column
    if j > 0:
        y, gamma, w = finish_image(j - 1, got[:, 1], us, ws, coeffs_before)
        w_out[...] = w
        ws = ws + [w_out]
        bend = head(us[j - 1][0], j)
        alpha = 4.0 * gamma * bend - 2.0 * head(y[0], j)
        summed = summed + alpha * (got[mine, 1] - bend * column_own)
        for k in range(j):
            x = x - us[k][...] * head(ws[k][0], j) - ws[k][...] * head(us[k][0], j)
    x = jnp.where(ids > j, x, 0.0)
    norm = jnp.sqrt(dot(x, x))
    denom = jnp.sqrt(2.0 * norm * (norm + head(x[0], j + 1)) + EPS)
    u = (x + jnp.where(ids == j + 1, norm, 0.0)) / denom
    u_out[...] = u
    image = (summed + norm * next_own) / denom
    for k in range(j):
        coeffs[k] = dot(ws[k][...], u)
        coeffs[K + k] = dot(us[k][...], u)
    if j == K - 1:
        send(payload, [image])
        return
    y_own = image
    x_own = next_own
    for k in range(j):
        u_own, w_own = us[k][mine], ws[k][mine]
        y_own = y_own - u_own * coeffs[k] - w_own * coeffs[K + k]
        x_own = x_own - u_own * head(ws[k][0], j + 1) - w_own * head(us[k][0], j + 1)
    x_own = x_own - 2.0 * head(u[0], j + 1) * y_own
    x_own = jnp.where(own_ids(mine) > j + 1, x_own, 0.0)
    x_ref[...] = x_own
    if j % 2:
        times_cols(tile, x_own, product)
        send(payload, [product[...], image, panel[j + 1], panel[j + 2]])
    else:
        times_rows(tile, x_ref, product)
        send(payload, [product[...], image])


ROWS = 128


def last_kernel(place, got, coeffs, *refs):
    us, ws = refs[:K], list(refs[K : 2 * K - 1])
    block, updated, images, w_ref, right, left = refs[2 * K - 1 :]
    row, col = place[0], place[1]

    @pl.when(pl.program_id(0) == 0)
    def _():
        _, _, w = finish_image(K - 1, got[:, 0], us, ws, coeffs)
        w_ref[...] = w
        all_ws = ws + [w_ref]
        for k in range(K):
            images[k] = all_ws[k][row]
            right[pl.ds(8 * k, 8), :] = all_ws[k][col]
            right[pl.ds(8 * (K + k), 8), :] = us[k][col]
        for a in range(8):
            lines = [v[row, a : a + 1] for v in [*us, *all_ws]]
            wide = jnp.concatenate([jnp.broadcast_to(v, (8, 128)) for v in lines], axis=0)
            left[a] = wide.T

    mask = jnp.where(
        slab_index((8, 128), 1) % 8 == slab_index((8, 128), 0), 1.0, 0.0
    )
    wide = left[pl.program_id(0)]
    spread = (wide[:, None, :] * mask[None, :, :]).reshape(ROWS * 8, 128)
    change = jnp.dot(spread, right[...], precision=lax.Precision.HIGHEST, preferred_element_type=F32)
    updated[...] = block[...] - change.reshape(ROWS, 8, 128)


def params():
    return pltpu.CompilerParams(vmem_limit_bytes=SCOPED)


def cost(flops, moved):
    return pl.CostEstimate(flops=flops, bytes_accessed=moved, transcendentals=0)


def exchange(payload, axis):
    return lax.all_to_all(payload, axis, split_axis=0, concat_axis=0, tiled=True)


def body(matrix):
    whole = jax.ShapeDtypeStruct((PEERS, 8, 128), F32)
    native = matrix.reshape(1024, 8, 128)
    place = jnp.stack([lax.axis_index("row"), lax.axis_index("col")]).astype(jnp.int32)
    panel = exchange(jnp.broadcast_to(native[None, : K + 1], (PEERS, K + 1, 8, 128)), "row")[0]
    tile = native.transpose(1, 0, 2)
    payload = pl.pallas_call(
        first_kernel,
        out_shape=jax.ShapeDtypeStruct((PEERS, 3, 8, 128), F32),
        in_specs=[smem(), vmem(), vmem()],
        out_specs=vmem(),
        scratch_shapes=[pltpu.VMEM((8, 128), F32)],
        compiler_params=params(),
        cost_estimate=cost(2**21, 2**22),
    )(place, panel, tile)
    us, ws, coeffs, before = [], [], None, None
    for j in range(K):
        got = exchange(payload, "row" if j % 2 else "col")
        inputs = [place, got, panel]
        if j % 2:
            inputs.append(before)
        if j < K - 1:
            inputs.append(tile)
        inputs += us + ws
        if j > 0:
            inputs.append(coeffs)
        sent = 1 if j == K - 1 else (4 if j % 2 else 2)
        outs = [jax.ShapeDtypeStruct((PEERS, sent, 8, 128), F32), whole, whole]
        if j > 0:
            outs.append(whole)
        results = pl.pallas_call(
            functools.partial(step_kernel, j),
            out_shape=outs,
            in_specs=[smem()] + [vmem()] * (len(inputs) - 1),
            out_specs=[vmem()] * len(outs),
            scratch_shapes=[pltpu.VMEM((8, 128), F32)] * 3,
            compiler_params=params(),
            cost_estimate=cost(2**21, 2**22),
            name=f"step_{j}",
        )(*inputs)
        payload, coeffs = results[0], results[2]
        us.append(results[1])
        if j > 0:
            ws.append(results[3])
        before = got
    got = exchange(payload, "col")
    fixed = lambda s: pl.BlockSpec(s, lambda i: (0,) * len(s))
    slab = fixed((PEERS, 8, 128))
    updated, images = pl.pallas_call(
        last_kernel,
        grid=(1024 // ROWS,),
        out_shape=(jax.ShapeDtypeStruct((1024, 8, 128), F32), jax.ShapeDtypeStruct((K, 8, 128), F32)),
        in_specs=[smem(), fixed((PEERS, 1, 8, 128)), slab]
        + [slab] * (2 * K - 1)
        + [pl.BlockSpec((ROWS, 8, 128), lambda i: (i, 0, 0))],
        out_specs=[pl.BlockSpec((ROWS, 8, 128), lambda i: (i, 0, 0)), fixed((K, 8, 128))],
        scratch_shapes=[
            pltpu.VMEM((PEERS, 8, 128), F32),
            pltpu.VMEM((128, 128), F32),
            pltpu.VMEM((8, 128, 128), F32),
        ],
        compiler_params=params(),
        cost_estimate=cost(2**25, 2**23),
    )(place, got, coeffs, *us, *ws, native)
    return updated.reshape(matrix.shape), images.reshape(K, 8, 1, 128)


def solution(mesh):
    spec = P(None, "row", None, None, "col", None)
    return jax.shard_map(
        body, mesh=mesh, in_specs=(spec,), out_specs=(spec, P(None, None, "row", None)), check_vma=False
    )
```

time: 955 us -> 165 us (0.17); the launches traced: 941 us -> 165 us
  blocking collectives: 426 us -> 119 us
  starting transfers between devices: 159 us -> 7.57 us
  matrix products: 129 us -> 0 us
  local copies, waits for them, and re-layouts: 109 us -> 8.85 us
  other arithmetic: 50.3 us -> 0.07 us
  waiting for transfers between devices: 43.5 us -> 6.03 us
  between operations: 23.6 us -> 0.7 us
  Pallas kernels: 0 us -> 22.9 us
    psum x46 -> x0, blocking collectives: 348 us -> none  [by_axis(): return functools.reduce(lax.psum, axes, value)]
    all_to_all x16 -> x1, starting transfers between devices: 159 us -> 7.57 us  [exchange(): lax.all_to_all(payload, axis, split_axis=0, concat_axis=0, tiled=True)]
    dot_general x88 -> x0, matrix products: 129 us -> none  [product(): return jnp.dot(left_side, right_side, precision=highest)]
    all_to_all x0 -> x9, blocking collectives: none -> 119 us  [exchange(): lax.all_to_all(payload, axis, split_axis=0, concat_axis=0, tiled=True)]
    all_gather x2 -> x0, blocking collectives: 78.5 us -> none  [from_root(): lax.all_gather(value, axis)]
    scatter x36 -> x0, local copies, waits for them, and re-layouts: 68.5 us -> none  [the longest x9 17.9 us: body(): images_cols = images_cols.at[:, position].set(update_c)]
    all_to_all x16 -> x1, waiting for transfers between devices: 43.5 us -> 6.03 us  [exchange(): lax.all_to_all(payload, axis, split_axis=0, concat_axis=0, tiled=True)]
    another operation x34 -> x1, other arithmetic: 31 us -> 0.07 us  [body(): jnp.stack([lax.axis_index('row'), lax.axis_index('col')]).astype(jnp.int32)]
  transfers between devices with their start and end apart: 16 -> 1, of which waited for: 13 -> 1; matrix products, arithmetic and copies ran while one was open for 10% -> 3% of each run, Pallas kernels for 0% -> 0%
where the time goes in v1:
time: 165 us
  blocking collectives  119 us (72%)
  Pallas kernels  22.9 us (14%)
  local copies, waits for them, and re-layouts  8.85 us (5%)
  starting transfers between devices  7.57 us (5%)
  waiting for transfers between devices  6.03 us (4%)
    all_to_all x9, blocking collectives, exchange(): lax.all_to_all(payload, axis, split_axis=0, concat_axis=0, tiled=True)  119 us
    pallas_call x8, Pallas kernels, body(): pl.pallas_call(functools.partial(step_kernel, j), out_shape=outs, in_spec...  14.3 us
    all_to_all x1, starting transfers between devices, exchange(): lax.all_to_all(payload, axis, split_axis=0, concat_axis=0, tiled=True)  7.57 us
    pallas_call x1, Pallas kernels, body(): pl.pallas_call(last_kernel, grid=(1024 // ROWS,), out_shape=(jax.ShapeDty...  7.04 us
    all_to_all x1, waiting for transfers between devices, exchange(): lax.all_to_all(payload, axis, split_axis=0, concat_axis=0, tiled=True)  6.03 us
    transpose x1, local copies, waits for them, and re-layouts, body(): tile = native.transpose(1, 0, 2)  5.01 us
  transfers between devices with their start and end apart: 1, of which 1 were waited for; matrix products, arithmetic and copies ran while one was open for 3% of the time, Pallas kernels for 0%

profile of v1, /device:TPU:1, one launch (start us, length us, event | category | flops | bytes accessed | tf_op | source)
XLA Modules:
  0.0 164.7 jit_solution(1873059406789529980)
XLA Ops:
  0.6 0.8 slice.8
  1.4 0.9 broadcast_in_dim.2
  2.3 7.6 %all-to-all-start = ((f32[16,9,8,128]{3,2,1,0:T(8,128)}), f32[16,9,8,128]{3,2,1,0:T(8,128)S(1)}, u32[]{:S(2)}, u32[]{:S(2)}) async-start(f32[16,9,8,128]{3,2,1,0:T(8,128)} %broadcast_in_dim.2), calls=%async_computation | async-start | bytes 1179648 | tf_op jit(solution)/shard_map/all_to_all | solution.py:201
  9.9 5.0 %copy.3.tile.refs_3_.refs_4_ = f32[8,1024,128]{2,1,0:T(8,128)} copy(f32[8,1024,128]{2,0,1:T(8,128)} %bitcast.14) | data formatting | bytes 8388608 | tf_op jit(solution)/shard_map/transpose | solution.py:209
  14.9 0.1 pad_add_fusion.place.refs_0_
  14.9 6.0 %all-to-all-done = f32[16,9,8,128]{3,2,1,0:T(8,128)S(1)} async-done(((f32[16,9,8,128]{3,2,1,0:T(8,128)}), f32[16,9,8,128]{3,2,1,0:T(8,128)S(1)}, u32[]{:S(2)}, u32[]{:S(2)}) %all-to-all-start) | async-done | bytes 589856 | tf_op jit(solution)/shard_map/all_to_all | solution.py:201
  21.0 0.0 copy-start
  21.0 2.2 %copy-done = f32[8,1024,128]{2,1,0:T(8,128)S(1)} copy-done((f32[8,1024,128]{2,1,0:T(8,128)S(1)}, f32[8,1024,128]{2,1,0:T(8,128)}, u32[]{:S(2)}) %copy-start) | copy-done | bytes 4194328
  23.2 1.5 shard_map.30
  24.7 20.5 %all_to_all.50.refs_1_.refs_3_ = f32[16,3,8,128]{3,2,1,0:T(8,128)S(1)} all-to-all(f32[16,3,8,128]{3,2,1,0:T(8,128)S(1)} %shard_map.30), channel_id=1, replica_groups=mesh['row'=16,'col'=16] {'col'}, dimensions={0} | all-to-all | bytes 393216 | tf_op jit(solution)/shard_map/all_to_all | solution.py:201
  45.2 1.6 step_0.1
  46.8 10.0 %all_to_all.51.refs_1_ = f32[16,2,8,128]{3,2,1,0:T(8,128)S(1)} all-to-all(f32[16,2,8,128]{3,2,1,0:T(8,128)S(1)} %get-tuple-element.35), channel_id=1, replica_groups=mesh['row'=16,'col'=16] {'row'}, dimensions={0} | all-to-all | bytes 262144 | tf_op jit(solution)/shard_map/all_to_all | solution.py:201
  56.9 1.9 %step_1.1 = (f32[16,4,8,128]{3,2,1,0:T(8,128)S(1)}, f32[16,8,128]{2,1,0:T(8,128)S(1)}, f32[16,8,128]{2,1,0:T(8,128)S(1)}, f32[16,8,128]{2,1,0:T(8,128)S(1)}) custom-call(s32[2]{0:T(128)S(1)} %pad_add_fusion.place.refs_0_, f32[16,2,8,128]{3,2,1,0:T(8,128)S(1)} %all_to_all.51.refs_1_, f32[9,8,128]{2,1,0:T(8,128)S(1)} %slice_bitcast_fusion.panel.refs_2_, ...), custom_call_target="tpu_custom_call" | custom-call | flops 2097152 | bytes 4194304 | tf_op jit(solution)/shard_map/step_1/pallas_call | solution.py:234
  58.8 15.3 %all_to_all.52.refs_1_.refs_3_ = f32[16,4,8,128]{3,2,1,0:T(8,128)S(1)} all-to-all(f32[16,4,8,128]{3,2,1,0:T(8,128)S(1)} %get-tuple-element.38), channel_id=1, replica_groups=mesh['row'=16,'col'=16] {'col'}, dimensions={0} | all-to-all | bytes 524288 | tf_op jit(solution)/shard_map/all_to_all | solution.py:201
  74.1 1.9 %step_2.1 = (f32[16,2,8,128]{3,2,1,0:T(8,128)S(1)}, f32[16,8,128]{2,1,0:T(8,128)S(1)}, f32[16,8,128]{2,1,0:T(8,128)S(1)}, f32[16,8,128]{2,1,0:T(8,128)S(1)}) custom-call(s32[2]{0:T(128)S(1)} %pad_add_fusion.place.refs_0_, f32[16,4,8,128]{3,2,1,0:T(8,128)S(1)} %all_to_all.52.refs_1_.refs_3_, f32[9,8,128]{2,1,0:T(8,128)S(1)} %slice_bitcast_fusion.panel.refs_2_, ...), custom_call_target="tpu_custom_call" | custom-call | flops 2097152 | bytes 4194304 | tf_op jit(solution)/shard_map/step_2/pallas_call | solution.py:234
  76.0 10.1 %all_to_all.53.refs_1_ = f32[16,2,8,128]{3,2,1,0:T(8,128)S(1)} all-to-all(f32[16,2,8,128]{3,2,1,0:T(8,128)S(1)} %get-tuple-element.42), channel_id=1, replica_groups=mesh['row'=16,'col'=16] {'row'}, dimensions={0} | all-to-all | bytes 262144 | tf_op jit(solution)/shard_map/all_to_all | solution.py:201
  86.1 2.0 %step_3.1 = (f32[16,4,8,128]{3,2,1,0:T(8,128)S(1)}, f32[16,8,128]{2,1,0:T(8,128)S(1)}, f32[16,8,128]{2,1,0:T(8,128)S(1)}, f32[16,8,128]{2,1,0:T(8,128)S(1)}) custom-call(s32[2]{0:T(128)S(1)} %pad_add_fusion.place.refs_0_, f32[16,2,8,128]{3,2,1,0:T(8,128)S(1)} %all_to_all.53.refs_1_, f32[9,8,128]{2,1,0:T(8,128)S(1)} %slice_bitcast_fusion.panel.refs_2_, ...), custom_call_target="tpu_custom_call" | custom-call | flops 2097152 | bytes 4194304 | tf_op jit(solution)/shard_map/step_3/pallas_call | solution.py:234
  88.1 15.3 %all_to_all.54.refs_1_.refs_3_ = f32[16,4,8,128]{3,2,1,0:T(8,128)S(1)} all-to-all(f32[16,4,8,128]{3,2,1,0:T(8,128)S(1)} %get-tuple-element.46), channel_id=1, replica_groups=mesh['row'=16,'col'=16] {'col'}, dimensions={0} | all-to-all | bytes 524288 | tf_op jit(solution)/shard_map/all_to_all | solution.py:201
  103.4 1.9 %step_4.1 = (f32[16,2,8,128]{3,2,1,0:T(8,128)S(1)}, f32[16,8,128]{2,1,0:T(8,128)S(1)}, f32[16,8,128]{2,1,0:T(8,128)S(1)}, f32[16,8,128]{2,1,0:T(8,128)S(1)}) custom-call(s32[2]{0:T(128)S(1)} %pad_add_fusion.place.refs_0_, f32[16,4,8,128]{3,2,1,0:T(8,128)S(1)} %all_to_all.54.refs_1_.refs_3_, f32[9,8,128]{2,1,0:T(8,128)S(1)} %slice_bitcast_fusion.panel.refs_2_, ...), custom_call_target="tpu_custom_call" | custom-call | flops 2097152 | bytes 4194304 | tf_op jit(solution)/shard_map/step_4/pallas_call | solution.py:234
  105.3 10.1 %all_to_all.55.refs_1_ = f32[16,2,8,128]{3,2,1,0:T(8,128)S(1)} all-to-all(f32[16,2,8,128]{3,2,1,0:T(8,128)S(1)} %get-tuple-element.50), channel_id=1, replica_groups=mesh['row'=16,'col'=16] {'row'}, dimensions={0} | all-to-all | bytes 262144 | tf_op jit(solution)/shard_map/all_to_all | solution.py:201
  115.4 2.0 %step_5.1 = (f32[16,4,8,128]{3,2,1,0:T(8,128)S(1)}, f32[16,8,128]{2,1,0:T(8,128)S(1)}, f32[16,8,128]{2,1,0:T(8,128)S(1)}, f32[16,8,128]{2,1,0:T(8,128)S(1)}) custom-call(s32[2]{0:T(128)S(1)} %pad_add_fusion.place.refs_0_, f32[16,2,8,128]{3,2,1,0:T(8,128)S(1)} %all_to_all.55.refs_1_, f32[9,8,128]{2,1,0:T(8,128)S(1)} %slice_bitcast_fusion.panel.refs_2_, ...), custom_call_target="tpu_custom_call" | custom-call | flops 2097152 | bytes 4194304 | tf_op jit(solution)/shard_map/step_5/pallas_call | solution.py:234
  117.4 0.0 copy-start.1
  117.4 15.6 %all_to_all.56.refs_1_.refs_3_ = f32[16,4,8,128]{3,2,1,0:T(8,128)S(1)} all-to-all(f32[16,4,8,128]{3,2,1,0:T(8,128)S(1)} %get-tuple-element.54), channel_id=1, replica_groups=mesh['row'=16,'col'=16] {'col'}, dimensions={0} | all-to-all | bytes 524288 | tf_op jit(solution)/shard_map/all_to_all | solution.py:201
  133.0 1.9 %step_6.1 = (f32[16,2,8,128]{3,2,1,0:T(8,128)S(1)}, f32[16,8,128]{2,1,0:T(8,128)S(1)}, f32[16,8,128]{2,1,0:T(8,128)S(1)}, f32[16,8,128]{2,1,0:T(8,128)S(1)}) custom-call(s32[2]{0:T(128)S(1)} %pad_add_fusion.place.refs_0_, f32[16,4,8,128]{3,2,1,0:T(8,128)S(1)} %all_to_all.56.refs_1_.refs_3_, f32[9,8,128]{2,1,0:T(8,128)S(1)} %slice_bitcast_fusion.panel.refs_2_, ...), custom_call_target="tpu_custom_call" | custom-call | flops 2097152 | bytes 4194304 | tf_op jit(solution)/shard_map/step_6/pallas_call | solution.py:234
  134.9 10.1 %all_to_all.57.refs_1_ = f32[16,2,8,128]{3,2,1,0:T(8,128)S(1)} all-to-all(f32[16,2,8,128]{3,2,1,0:T(8,128)S(1)} %get-tuple-element.58), channel_id=1, replica_groups=mesh['row'=16,'col'=16] {'row'}, dimensions={0} | all-to-all | bytes 262144 | tf_op jit(solution)/shard_map/all_to_all | solution.py:201
  145.0 1.1 step_7.1
  146.2 11.5 %all_to_all.58.got = f32[16,1,8,128]{3,2,1,0:T(8,128)S(1)} all-to-all(f32[16,1,8,128]{3,2,1,0:T(8,128)S(1)} %get-tuple-element.62), channel_id=1, replica_groups=mesh['row'=16,'col'=16] {'col'}, dimensions={0} | all-to-all | bytes 131072 | tf_op jit(solution)/shard_map/all_to_all | solution.py:201
  157.6 0.0 copy-done.1
  157.6 7.0 %shard_map.31 = (f32[1024,8,128]{2,1,0:T(8,128)}, f32[8,8,128]{2,1,0:T(8,128)}) custom-call(s32[2]{0:T(128)S(1)} %pad_add_fusion.place.refs_0_, f32[16,1,8,128]{3,2,1,0:T(8,128)S(1)} %all_to_all.58.got, f32[16,8,128]{2,1,0:T(8,128)S(1)} %get-tuple-element.63.coeffs, f32[16,8,128]{2,1,0:T(8,128)S(1)} %get-tuple-element.36.refs_5_.refs_4_.refs_0_, ...), custom_call_target="tpu_custom_call" | custom-call | flops 33554432 | bytes 8388608 | tf_op jit(solution)/shard_map/pallas_call | solution.py:252
  (1 shorter events, 0.0 us)
Async XLA Ops:
  2.3 18.7 %all-to-all-start = ((f32[16,9,8,128]{3,2,1,0:T(8,128)}), f32[16,9,8,128]{3,2,1,0:T(8,128)S(1)}, u32[]{:S(2)}, u32[]{:S(2)}) async-start(f32[16,9,8,128]{3,2,1,0:T(8,128)} %broadcast_in_dim.2), calls=%async_computation | async-start | bytes 1179648 | tf_op jit(solution)/shard_map/all_to_all | solution.py:201
  21.0 2.2 %copy-start = (f32[8,1024,128]{2,1,0:T(8,128)S(1)}, f32[8,1024,128]{2,1,0:T(8,128)}, u32[]{:S(2)}) copy-start(f32[8,1024,128]{2,1,0:T(8,128)} %copy.3.tile.refs_3_.refs_4_) | copy-start | bytes 12582916
  117.4 40.2 %copy-start.1 = (f32[8,1,128,8,1,128]{5,4,3,2,1,0:T(1,128)S(1)}, f32[8,1,128,8,1,128]{5,4,3,2,1,0:T(1,128)}, u32[]{:S(2)}) copy-start(f32[8,1,128,8,1,128]{5,4,3,2,1,0:T(1,128)} %param.1) | copy-start | bytes 12582916

commit v2 on v1

--- a/solution.py
+++ b/solution.py
@@ -12,6 +12,7 @@
 PEERS = 16
 F32 = jnp.float32
 SCOPED = 16 * 1024 * 1024
+WIDE = 62000000
 
 
 def vmem():
@@ -83,10 +84,60 @@
             payload[q, n] = slab
 
 
-def first_kernel(place, panel, tile, payload, product):
-    x = jnp.where(own_ids(place[1]) > 0, panel[0], 0.0)
-    times_cols(tile, x, product)
-    send(payload, [product[...], panel[0], panel[1]])
+def panel_kernel(matrix, payload, corner, panel, sem):
+    copies = []
+    for a in range(8):
+        rows = pl.ds(128 * a, 128)
+        copies.append(pltpu.make_async_copy(matrix.at[rows, 0, :], corner.at[rows], sem.at[a]))
+        copies[-1].start()
+    for a in range(8):
+        copies[a].wait()
+        lines = corner[pl.ds(128 * a, 128), :].T
+        for k in range(K + 1):
+            panel[k, a : a + 1, :] = lines[k : k + 1, :]
+    for q in range(PEERS):
+        payload[q, 0] = panel[0]
+        payload[q, 1] = panel[1]
+        payload[q, 2] = panel[2 + q % (K - 1)]
+
+
+def load_kernel(matrix, tile, spare, held, fetched, stored):
+    into = [pltpu.make_async_copy(matrix.at[:, b, :], held.at[b], fetched.at[b]) for b in range(8)]
+    out = [
+        pltpu.make_async_copy(held.at[b], ref.at[b], stored.at[n, b])
+        for b in range(8)
+        for n, ref in enumerate((tile, spare))
+    ]
+    for copy in into:
+        copy.start()
+    for b in range(8):
+        into[b].wait()
+        out[2 * b].start()
+        out[2 * b + 1].start()
+    for copy in out:
+        copy.wait()
+
+
+def first_kernel(place, panel, tile, payload, held, x_ref, lines, sem):
+    copies = [pltpu.make_async_copy(tile.at[b], held.at[b], sem.at[b]) for b in range(8)]
+    for copy in copies:
+        copy.start()
+    x_ref[...] = jnp.where(own_ids(place[0]) > 0, panel[0, 0], 0.0)
+    for a in range(8):
+        lines[pl.ds(128 * a, 128), :] = jnp.broadcast_to(x_ref[a : a + 1, :], (128, 128)).T
+    for b in range(8):
+        copies[b].wait()
+
+        def rows(a, acc):
+            at = pl.ds(pl.multiple_of(a * 128, 128), 128)
+            return acc + jnp.sum((held[b, at, :] * lines[at, :]).reshape(16, 8, 128), axis=0)
+
+        line = jnp.sum(lax.fori_loop(0, 8, rows, jnp.zeros((8, 128), F32)), axis=0, keepdims=True)
+        for q in range(PEERS):
+            payload[q, 0, b : b + 1, :] = line
+    for q in range(PEERS):
+        payload[q, 1] = panel[0, 0]
+        payload[q, 2] = panel[0, 1]
 
 
 def finish_image(j, got, us, ws, coeffs):
@@ -99,8 +150,9 @@
 
 def step_kernel(j, *refs):
     refs = list(refs)
-    place, got, panel = refs[:3]
-    del refs[:3]
+    place, got = refs[:2]
+    del refs[:2]
+    spare = got if j == 1 else refs.pop(0) if j == 0 or j % 2 else None
     late = refs.pop(0) if j % 2 else got
     tile = refs.pop(0) if j < K - 1 else None
     us = [refs.pop(0) for _ in range(j)]
@@ -110,15 +162,15 @@
     del refs[:3]
     if j > 0:
         w_out = refs.pop(0)
-    y_ref, x_ref, product = refs
-    mine = place[j % 2]
+    x_ref, product = refs
+    mine = place[(j + 1) % 2]
     ids = full_ids()
     summed = got[0, 0]
     for q in range(1, PEERS):
         summed = summed + got[q, 0]
     at = {0: 1, 1: 2}.get(j, 3 if j % 2 else 2)
     column, column_own = late[:, at], late[mine, at]
-    next_own = panel[j + 1] if j % 2 else late[mine, at + 1]
+    next_own = spare[j - 1, 2] if j % 2 else late[mine, at + 1]
     x = column
     if j > 0:
         y, gamma, w = finish_image(j - 1, got[:, 1], us, ws, coeffs_before)
@@ -151,46 +203,53 @@
     x_own = jnp.where(own_ids(mine) > j + 1, x_own, 0.0)
     x_ref[...] = x_own
     if j % 2:
+        times_rows(tile, x_ref, product)
+        send(payload, [product[...], image, spare[j - 1, 2], spare[j, 2]])
+    else:
         times_cols(tile, x_own, product)
-        send(payload, [product[...], image, panel[j + 1], panel[j + 2]])
-    else:
-        times_rows(tile, x_ref, product)
-        send(payload, [product[...], image])
-
-
-ROWS = 128
+        send(payload, [product[...], image] + ([spare[0, 2]] if j == 0 else []))
+
+
+def thirds(value):
+    high = value.astype(jnp.bfloat16).astype(F32)
+    rest = value - high
+    middle = rest.astype(jnp.bfloat16).astype(F32)
+    return high, middle, rest - middle
 
 
 def last_kernel(place, got, coeffs, *refs):
     us, ws = refs[:K], list(refs[K : 2 * K - 1])
-    block, updated, images, w_ref, right, left = refs[2 * K - 1 :]
+    tile, updated, images, w_ref, right, result, sem = refs[2 * K - 1 :]
     row, col = place[0], place[1]
-
-    @pl.when(pl.program_id(0) == 0)
-    def _():
-        _, _, w = finish_image(K - 1, got[:, 0], us, ws, coeffs)
-        w_ref[...] = w
-        all_ws = ws + [w_ref]
-        for k in range(K):
-            images[k] = all_ws[k][row]
-            right[pl.ds(8 * k, 8), :] = all_ws[k][col]
-            right[pl.ds(8 * (K + k), 8), :] = us[k][col]
-        for a in range(8):
-            lines = [v[row, a : a + 1] for v in [*us, *all_ws]]
-            wide = jnp.concatenate([jnp.broadcast_to(v, (8, 128)) for v in lines], axis=0)
-            left[a] = wide.T
-
-    mask = jnp.where(
-        slab_index((8, 128), 1) % 8 == slab_index((8, 128), 0), 1.0, 0.0
-    )
-    wide = left[pl.program_id(0)]
-    spread = (wide[:, None, :] * mask[None, :, :]).reshape(ROWS * 8, 128)
-    change = jnp.dot(spread, right[...], precision=lax.Precision.HIGHEST, preferred_element_type=F32)
-    updated[...] = block[...] - change.reshape(ROWS, 8, 128)
-
-
-def params():
-    return pltpu.CompilerParams(vmem_limit_bytes=SCOPED)
+    _, _, w = finish_image(K - 1, got[:, 0], us, ws, coeffs)
+    w_ref[...] = w
+    ws = ws + [w_ref]
+    for k in range(K):
+        images[k] = ws[k][row]
+    pad = jnp.zeros((32, 128), F32)
+    for b in range(8):
+        high, middle, low = thirds(jnp.concatenate([v[col, b : b + 1] for v in [*ws, *us]], axis=0))
+        right[:, 128 * b : 128 * (b + 1)] = jnp.concatenate(
+            [high, middle, high, low, middle, high, pad], axis=0
+        ).astype(jnp.bfloat16)
+    copies = []
+    for a in range(8):
+        high, middle, low = thirds(jnp.concatenate([v[row, a : a + 1] for v in [*us, *ws]], axis=0))
+        left = jnp.concatenate([high, high, middle, high, middle, low, pad], axis=0).T.astype(jnp.bfloat16)
+        change = jnp.dot(left, right[...], preferred_element_type=F32)
+        for b in range(8):
+            rows = pl.ds(128 * a, 128)
+            result[b, rows, :] = tile[b, rows, :] - change[:, 128 * b : 128 * (b + 1)]
+            copies.append(
+                pltpu.make_async_copy(result.at[b, rows, :], updated.at[rows, b, :], sem.at[8 * a + b])
+            )
+            copies[-1].start()
+    for copy in copies:
+        copy.wait()
+
+
+def params(limit=SCOPED):
+    return pltpu.CompilerParams(vmem_limit_bytes=limit)
 
 
 def cost(flops, moved):
@@ -205,21 +264,63 @@
     whole = jax.ShapeDtypeStruct((PEERS, 8, 128), F32)
     native = matrix.reshape(1024, 8, 128)
     place = jnp.stack([lax.axis_index("row"), lax.axis_index("col")]).astype(jnp.int32)
-    panel = exchange(jnp.broadcast_to(native[None, : K + 1], (PEERS, K + 1, 8, 128)), "row")[0]
-    tile = native.transpose(1, 0, 2)
+    hbm = pl.BlockSpec(memory_space=pltpu.HBM)
     payload = pl.pallas_call(
+        panel_kernel,
+        out_shape=jax.ShapeDtypeStruct((PEERS, 3, 8, 128), F32),
+        in_specs=[hbm],
+        out_specs=vmem(),
+        scratch_shapes=[
+            pltpu.VMEM((1024, 128), F32),
+            pltpu.VMEM((K + 1, 8, 128), F32),
+            pltpu.SemaphoreType.DMA((8,)),
+        ],
+        compiler_params=params(WIDE),
+        cost_estimate=cost(2**20, 2**20),
+    )(native)
+    panel = exchange(payload, "col")
+    streamed, plain = pl.pallas_call(
+        load_kernel,
+        out_shape=(
+            jax.ShapeDtypeStruct((40, 1024, 128), F32),
+            jax.ShapeDtypeStruct((8, 1024, 128), F32),
+        ),
+        in_specs=[hbm],
+        out_specs=[hbm, hbm],
+        scratch_shapes=[
+            pltpu.VMEM((8, 1024, 128), F32),
+            pltpu.SemaphoreType.DMA((8,)),
+            pltpu.SemaphoreType.DMA((2, 8)),
+        ],
+        compiler_params=params(WIDE),
+        cost_estimate=cost(2**21, 2**23),
+    )(native)
+    payload, tile = pl.pallas_call(
         first_kernel,
-        out_shape=jax.ShapeDtypeStruct((PEERS, 3, 8, 128), F32),
-        in_specs=[smem(), vmem(), vmem()],
-        out_specs=vmem(),
-        scratch_shapes=[pltpu.VMEM((8, 128), F32)],
-        compiler_params=params(),
+        out_shape=(
+            jax.ShapeDtypeStruct((PEERS, 3, 8, 128), F32),
+            jax.ShapeDtypeStruct((8, 1024, 128), F32),
+        ),
+        in_specs=[smem(), vmem(), hbm],
+        out_specs=[vmem(), vmem()],
+        scratch_shapes=[
+            pltpu.VMEM((8, 128), F32),
+            pltpu.VMEM((1024, 128), F32),
+            pltpu.SemaphoreType.DMA((8,)),
+        ],
+        compiler_params=params(48000000),
         cost_estimate=cost(2**21, 2**22),
-    )(place, panel, tile)
+    )(place, panel, streamed)
     us, ws, coeffs, before = [], [], None, None
     for j in range(K):
-        got = exchange(payload, "row" if j % 2 else "col")
-        inputs = [place, got, panel]
+        got = exchange(payload, "col" if j % 2 else "row")
+        inputs = [place, got]
+        if j == 0:
+            inputs.append(panel)
+        if j == 1:
+            spare = got
+        elif j % 2:
+            inputs.append(spare)
         if j % 2:
             inputs.append(before)
         if j < K - 1:
@@ -227,7 +328,7 @@
         inputs += us + ws
         if j > 0:
             inputs.append(coeffs)
-        sent = 1 if j == K - 1 else (4 if j % 2 else 2)
+        sent = 1 if j == K - 1 else 3 if j == 0 else 4 if j % 2 else 2
         outs = [jax.ShapeDtypeStruct((PEERS, sent, 8, 128), F32), whole, whole]
         if j > 0:
             outs.append(whole)
@@ -236,7 +337,7 @@
             out_shape=outs,
             in_specs=[smem()] + [vmem()] * (len(inputs) - 1),
             out_specs=[vmem()] * len(outs),
-            scratch_shapes=[pltpu.VMEM((8, 128), F32)] * 3,
+            scratch_shapes=[pltpu.VMEM((8, 128), F32)] * 2,
             compiler_params=params(),
             cost_estimate=cost(2**21, 2**22),
             name=f"step_{j}",
@@ -246,25 +347,21 @@
         if j > 0:
             ws.append(results[3])
         before = got
-    got = exchange(payload, "col")
-    fixed = lambda s: pl.BlockSpec(s, lambda i: (0,) * len(s))
-    slab = fixed((PEERS, 8, 128))
+    got = exchange(payload, "row")
     updated, images = pl.pallas_call(
         last_kernel,
-        grid=(1024 // ROWS,),
         out_shape=(jax.ShapeDtypeStruct((1024, 8, 128), F32), jax.ShapeDtypeStruct((K, 8, 128), F32)),
-        in_specs=[smem(), fixed((PEERS, 1, 8, 128)), slab]
-        + [slab] * (2 * K - 1)
-        + [pl.BlockSpec((ROWS, 8, 128), lambda i: (i, 0, 0))],
-        out_specs=[pl.BlockSpec((ROWS, 8, 128), lambda i: (i, 0, 0)), fixed((K, 8, 128))],
+        in_specs=[smem()] + [vmem()] * (2 * K + 2),
+        out_specs=[hbm, vmem()],
         scratch_shapes=[
             pltpu.VMEM((PEERS, 8, 128), F32),
-            pltpu.VMEM((128, 128), F32),
-            pltpu.VMEM((8, 128, 128), F32),
+            pltpu.VMEM((128, 1024), jnp.bfloat16),
+            pltpu.VMEM((8, 1024, 128), F32),
+            pltpu.SemaphoreType.DMA((64,)),
         ],
         compiler_params=params(),
         cost_estimate=cost(2**25, 2**23),
-    )(place, got, coeffs, *us, *ws, native)
+    )(place, got, coeffs, *us, *ws, plain)
     return updated.reshape(matrix.shape), images.reshape(K, 8, 1, 128)
 
 

time: 165 us -> 154 us (0.933)
  blocking collectives: 119 us -> 109 us
  local copies, waits for them, and re-layouts: 8.85 us -> 0.01 us
  Pallas kernels: 22.9 us -> 28.4 us
  starting transfers between devices: 7.57 us -> 9.98 us
    all_to_all x9, blocking collectives: 119 us -> 109 us  [exchange(): lax.all_to_all(payload, axis, split_axis=0, concat_axis=0, tiled=True)]
    pallas_call x2 -> x4, Pallas kernels: 8.54 us -> 14 us  [the longest x1 4.52 us: body(): pl.pallas_call(load_kernel, out_shape=(jax.ShapeDtypeStruct((40, 1024, 12...]
    transpose x1 -> x0, local copies, waits for them, and re-layouts: 5.01 us -> none  [body(): tile = native.transpose(1, 0, 2)]
    all_to_all x1, starting transfers between devices: 7.57 us -> 9.98 us  [exchange(): lax.all_to_all(payload, axis, split_axis=0, concat_axis=0, tiled=True)]
    unnamed x4 -> x2, local copies, waits for them, and re-layouts: 2.19 us -> 0.01 us
  transfers between devices with their start and end apart: 1 -> 1, of which waited for: 1 -> 1; matrix products, arithmetic and copies ran while one was open for 3% -> 0% of each run, Pallas kernels for 0% -> 3%
where the time goes in v2:
time: 154 us
  blocking collectives  109 us (71%)
  Pallas kernels  28.4 us (18%)
  starting transfers between devices  9.98 us (6%)
  waiting for transfers between devices  5.59 us (4%)
    all_to_all x9, blocking collectives, exchange(): lax.all_to_all(payload, axis, split_axis=0, concat_axis=0, tiled=True)  109 us
    pallas_call x8, Pallas kernels, body(): pl.pallas_call(functools.partial(step_kernel, j), out_shape=outs, in_spec...  14.4 us
    all_to_all x1, starting transfers between devices, exchange(): lax.all_to_all(payload, axis, split_axis=0, concat_axis=0, tiled=True)  9.98 us
    all_to_all x1, waiting for transfers between devices, exchange(): lax.all_to_all(payload, axis, split_axis=0, concat_axis=0, tiled=True)  5.59 us
    pallas_call x1, Pallas kernels, body(): pl.pallas_call(load_kernel, out_shape=(jax.ShapeDtypeStruct((40, 1024, 12...  4.52 us
    pallas_call x1, Pallas kernels, body(): pl.pallas_call(last_kernel, out_shape=(jax.ShapeDtypeStruct((1024, 8, 128...  4.12 us
    pallas_call x1, Pallas kernels, body(): pl.pallas_call(first_kernel, out_shape=(jax.ShapeDtypeStruct((PEERS, 3, 8...  3.23 us
  transfers between devices with their start and end apart: 1, of which 1 were waited for; matrix products, arithmetic and copies ran while one was open for 0% of the time, Pallas kernels for 3%

profile of v2, /device:TPU:1, one launch (start us, length us, event | category | flops | bytes accessed | tf_op | source)
XLA Modules:
  0.0 153.9 jit_solution(4618986095488052104)
XLA Ops:
  0.6 2.2 %shard_map.30 = f32[16,3,8,128]{3,2,1,0:T(8,128)} custom-call(f32[1024,8,128]{2,1,0:T(8,128)} %bitcast.9), custom_call_target="tpu_custom_call" | custom-call | flops 1048576 | bytes 1048576 | tf_op jit(solution)/shard_map/pallas_call | solution.py:268
  2.8 10.0 %all-to-all-start = ((f32[16,3,8,128]{3,2,1,0:T(8,128)}), f32[16,3,8,128]{3,2,1,0:T(8,128)S(1)}, u32[]{:S(2)}, u32[]{:S(2)}) async-start(f32[16,3,8,128]{3,2,1,0:T(8,128)} %shard_map.30), calls=%async_computation | async-start | bytes 393216 | tf_op jit(solution)/shard_map/all_to_all | solution.py:260
  12.8 4.5 %shard_map.31 = (f32[40,1024,128]{2,1,0:T(8,128)}, f32[8,1024,128]{2,1,0:T(8,128)}) custom-call(f32[1024,8,128]{2,1,0:T(8,128)} %bitcast.10), custom_call_target="tpu_custom_call" | custom-call | flops 2097152 | bytes 8388608 | tf_op jit(solution)/shard_map/pallas_call | solution.py:282
  17.3 0.1 pad_add_fusion.place.refs_0_
  17.4 5.6 %all-to-all-done.panel.refs_2_ = f32[16,3,8,128]{3,2,1,0:T(8,128)S(1)} async-done(((f32[16,3,8,128]{3,2,1,0:T(8,128)}), f32[16,3,8,128]{3,2,1,0:T(8,128)S(1)}, u32[]{:S(2)}, u32[]{:S(2)}) %all-to-all-start) | async-done | bytes 196640 | tf_op jit(solution)/shard_map/all_to_all | solution.py:260
  23.0 3.2 %shard_map.32 = (f32[16,3,8,128]{3,2,1,0:T(8,128)S(1)}, f32[8,1024,128]{2,1,0:T(8,128)S(1)}) custom-call(s32[2]{0:T(128)S(1)} %pad_add_fusion.place.refs_0_, f32[16,3,8,128]{3,2,1,0:T(8,128)S(1)} %all-to-all-done.panel.refs_2_, f32[40,1024,128]{2,1,0:T(8,128)} %get-tuple-element.39.tile), custom_call_target="tpu_custom_call" | custom-call | flops 2097152 | bytes 4194304 | tf_op jit(solution)/shard_map/pallas_call | solution.py:298
  26.2 14.5 %all_to_all.50.refs_1_.refs_2_ = f32[16,3,8,128]{3,2,1,0:T(8,128)S(1)} all-to-all(f32[16,3,8,128]{3,2,1,0:T(8,128)S(1)} %get-tuple-element.40), channel_id=1, replica_groups=mesh['row'=16,'col'=16] {'row'}, dimensions={0} | all-to-all | bytes 393216 | tf_op jit(solution)/shard_map/all_to_all | solution.py:260
  40.8 1.7 %step_0.1 = (f32[16,3,8,128]{3,2,1,0:T(8,128)S(1)}, f32[16,8,128]{2,1,0:T(8,128)S(1)}, f32[16,8,128]{2,1,0:T(8,128)S(1)}) custom-call(s32[2]{0:T(128)S(1)} %pad_add_fusion.place.refs_0_, f32[16,3,8,128]{3,2,1,0:T(8,128)S(1)} %all_to_all.50.refs_1_.refs_2_, f32[16,3,8,128]{3,2,1,0:T(8,128)S(1)} %all-to-all-done.panel.refs_2_, ...), custom_call_target="tpu_custom_call" | custom-call | flops 2097152 | bytes 4194304 | tf_op jit(solution)/shard_map/step_0/pallas_call | solution.py:335
  42.5 13.3 %all_to_all.51.refs_1_.refs_2_ = f32[16,3,8,128]{3,2,1,0:T(8,128)S(1)} all-to-all(f32[16,3,8,128]{3,2,1,0:T(8,128)S(1)} %get-tuple-element.42), channel_id=1, replica_groups=mesh['row'=16,'col'=16] {'col'}, dimensions={0} | all-to-all | bytes 393216 | tf_op jit(solution)/shard_map/all_to_all | solution.py:260
  55.8 1.9 %step_1.1 = (f32[16,4,8,128]{3,2,1,0:T(8,128)S(1)}, f32[16,8,128]{2,1,0:T(8,128)S(1)}, f32[16,8,128]{2,1,0:T(8,128)S(1)}, f32[16,8,128]{2,1,0:T(8,128)S(1)}) custom-call(s32[2]{0:T(128)S(1)} %pad_add_fusion.place.refs_0_, f32[16,3,8,128]{3,2,1,0:T(8,128)S(1)} %all_to_all.51.refs_1_.refs_2_, f32[16,3,8,128]{3,2,1,0:T(8,128)S(1)} %all_to_all.50.refs_1_.refs_2_, ...), custom_call_target="tpu_custom_call" | custom-call | flops 2097152 | bytes 4194304 | tf_op jit(solution)/shard_map/step_1/pallas_call | solution.py:335
  57.7 11.3 %all_to_all.52.refs_1_.refs_3_ = f32[16,4,8,128]{3,2,1,0:T(8,128)S(1)} all-to-all(f32[16,4,8,128]{3,2,1,0:T(8,128)S(1)} %get-tuple-element.45), channel_id=1, replica_groups=mesh['row'=16,'col'=16] {'row'}, dimensions={0} | all-to-all | bytes 524288 | tf_op jit(solution)/shard_map/all_to_all | solution.py:260
  69.0 1.9 %step_2.1 = (f32[16,2,8,128]{3,2,1,0:T(8,128)S(1)}, f32[16,8,128]{2,1,0:T(8,128)S(1)}, f32[16,8,128]{2,1,0:T(8,128)S(1)}, f32[16,8,128]{2,1,0:T(8,128)S(1)}) custom-call(s32[2]{0:T(128)S(1)} %pad_add_fusion.place.refs_0_, f32[16,4,8,128]{3,2,1,0:T(8,128)S(1)} %all_to_all.52.refs_1_.refs_3_, f32[8,1024,128]{2,1,0:T(8,128)S(1)} %get-tuple-element.41.refs_3_.refs_2_.refs_4_, ...), custom_call_target="tpu_custom_call" | custom-call | flops 2097152 | bytes 4194304 | tf_op jit(solution)/shard_map/step_2/pallas_call | solution.py:335
  70.9 12.6 %all_to_all.53.refs_1_ = f32[16,2,8,128]{3,2,1,0:T(8,128)S(1)} all-to-all(f32[16,2,8,128]{3,2,1,0:T(8,128)S(1)} %get-tuple-element.49), channel_id=1, replica_groups=mesh['row'=16,'col'=16] {'col'}, dimensions={0} | all-to-all | bytes 262144 | tf_op jit(solution)/shard_map/all_to_all | solution.py:260
  83.5 1.9 %step_3.1 = (f32[16,4,8,128]{3,2,1,0:T(8,128)S(1)}, f32[16,8,128]{2,1,0:T(8,128)S(1)}, f32[16,8,128]{2,1,0:T(8,128)S(1)}, f32[16,8,128]{2,1,0:T(8,128)S(1)}) custom-call(s32[2]{0:T(128)S(1)} %pad_add_fusion.place.refs_0_, f32[16,2,8,128]{3,2,1,0:T(8,128)S(1)} %all_to_all.53.refs_1_, f32[16,3,8,128]{3,2,1,0:T(8,128)S(1)} %all_to_all.51.refs_1_.refs_2_, ...), custom_call_target="tpu_custom_call" | custom-call | flops 2097152 | bytes 4194304 | tf_op jit(solution)/shard_map/step_3/pallas_call | solution.py:335
  85.4 11.2 %all_to_all.54.refs_1_.refs_3_ = f32[16,4,8,128]{3,2,1,0:T(8,128)S(1)} all-to-all(f32[16,4,8,128]{3,2,1,0:T(8,128)S(1)} %get-tuple-element.53), channel_id=1, replica_groups=mesh['row'=16,'col'=16] {'row'}, dimensions={0} | all-to-all | bytes 524288 | tf_op jit(solution)/shard_map/all_to_all | solution.py:260
  96.6 2.0 %step_4.1 = (f32[16,2,8,128]{3,2,1,0:T(8,128)S(1)}, f32[16,8,128]{2,1,0:T(8,128)S(1)}, f32[16,8,128]{2,1,0:T(8,128)S(1)}, f32[16,8,128]{2,1,0:T(8,128)S(1)}) custom-call(s32[2]{0:T(128)S(1)} %pad_add_fusion.place.refs_0_, f32[16,4,8,128]{3,2,1,0:T(8,128)S(1)} %all_to_all.54.refs_1_.refs_3_, f32[8,1024,128]{2,1,0:T(8,128)S(1)} %get-tuple-element.41.refs_3_.refs_2_.refs_4_, ...), custom_call_target="tpu_custom_call" | custom-call | flops 2097152 | bytes 4194304 | tf_op jit(solution)/shard_map/step_4/pallas_call | solution.py:335
  98.5 12.7 %all_to_all.55.refs_1_ = f32[16,2,8,128]{3,2,1,0:T(8,128)S(1)} all-to-all(f32[16,2,8,128]{3,2,1,0:T(8,128)S(1)} %get-tuple-element.57), channel_id=1, replica_groups=mesh['row'=16,'col'=16] {'col'}, dimensions={0} | all-to-all | bytes 262144 | tf_op jit(solution)/shard_map/all_to_all | solution.py:260
  111.2 1.9 %step_5.1 = (f32[16,4,8,128]{3,2,1,0:T(8,128)S(1)}, f32[16,8,128]{2,1,0:T(8,128)S(1)}, f32[16,8,128]{2,1,0:T(8,128)S(1)}, f32[16,8,128]{2,1,0:T(8,128)S(1)}) custom-call(s32[2]{0:T(128)S(1)} %pad_add_fusion.place.refs_0_, f32[16,2,8,128]{3,2,1,0:T(8,128)S(1)} %all_to_all.55.refs_1_, f32[16,3,8,128]{3,2,1,0:T(8,128)S(1)} %all_to_all.51.refs_1_.refs_2_, ...), custom_call_target="tpu_custom_call" | custom-call | flops 2097152 | bytes 4194304 | tf_op jit(solution)/shard_map/step_5/pallas_call | solution.py:335
  113.2 0.0 copy-start
  113.2 11.4 %all_to_all.56.refs_1_.refs_3_ = f32[16,4,8,128]{3,2,1,0:T(8,128)S(1)} all-to-all(f32[16,4,8,128]{3,2,1,0:T(8,128)S(1)} %get-tuple-element.61), channel_id=1, replica_groups=mesh['row'=16,'col'=16] {'row'}, dimensions={0} | all-to-all | bytes 524288 | tf_op jit(solution)/shard_map/all_to_all | solution.py:260
  124.6 2.0 %step_6.1 = (f32[16,2,8,128]{3,2,1,0:T(8,128)S(1)}, f32[16,8,128]{2,1,0:T(8,128)S(1)}, f32[16,8,128]{2,1,0:T(8,128)S(1)}, f32[16,8,128]{2,1,0:T(8,128)S(1)}) custom-call(s32[2]{0:T(128)S(1)} %pad_add_fusion.place.refs_0_, f32[16,4,8,128]{3,2,1,0:T(8,128)S(1)} %all_to_all.56.refs_1_.refs_3_, f32[8,1024,128]{2,1,0:T(8,128)S(1)} %get-tuple-element.41.refs_3_.refs_2_.refs_4_, ...), custom_call_target="tpu_custom_call" | custom-call | flops 2097152 | bytes 4194304 | tf_op jit(solution)/shard_map/step_6/pallas_call | solution.py:335
  126.6 12.7 %all_to_all.57.refs_1_ = f32[16,2,8,128]{3,2,1,0:T(8,128)S(1)} all-to-all(f32[16,2,8,128]{3,2,1,0:T(8,128)S(1)} %get-tuple-element.65), channel_id=1, replica_groups=mesh['row'=16,'col'=16] {'col'}, dimensions={0} | all-to-all | bytes 262144 | tf_op jit(solution)/shard_map/all_to_all | solution.py:260
  139.3 1.1 step_7.1
  140.4 9.4 %all_to_all.58.got = f32[16,1,8,128]{3,2,1,0:T(8,128)S(1)} all-to-all(f32[16,1,8,128]{3,2,1,0:T(8,128)S(1)} %get-tuple-element.69), channel_id=1, replica_groups=mesh['row'=16,'col'=16] {'row'}, dimensions={0} | all-to-all | bytes 131072 | tf_op jit(solution)/shard_map/all_to_all | solution.py:260
  149.8 0.0 copy-done
  149.8 4.1 %shard_map.33 = (f32[1024,8,128]{2,1,0:T(8,128)}, f32[8,8,128]{2,1,0:T(8,128)}) custom-call(s32[2]{0:T(128)S(1)} %pad_add_fusion.place.refs_0_, f32[16,1,8,128]{3,2,1,0:T(8,128)S(1)} %all_to_all.58.got, f32[16,8,128]{2,1,0:T(8,128)S(1)} %get-tuple-element.70.coeffs, f32[16,8,128]{2,1,0:T(8,128)S(1)} %get-tuple-element.43.refs_4_.refs_3_.refs_5_.refs_0_, ...), custom_call_target="tpu_custom_call" | custom-call | flops 33554432 | bytes 8388608 | tf_op jit(solution)/shard_map/pallas_call | solution.py:351
Async XLA Ops:
  2.8 20.2 %all-to-all-start = ((f32[16,3,8,128]{3,2,1,0:T(8,128)}), f32[16,3,8,128]{3,2,1,0:T(8,128)S(1)}, u32[]{:S(2)}, u32[]{:S(2)}) async-start(f32[16,3,8,128]{3,2,1,0:T(8,128)} %shard_map.30), calls=%async_computation | async-start | bytes 393216 | tf_op jit(solution)/shard_map/all_to_all | solution.py:260
  113.2 36.6 %copy-start = (f32[8,1024,128]{2,1,0:T(8,128)S(1)}, f32[8,1024,128]{2,1,0:T(8,128)}, u32[]{:S(2)}) copy-start(f32[8,1024,128]{2,1,0:T(8,128)} %get-tuple-element.73.refs_15_) | copy-start | bytes 12582916

commit v3 on v2

--- a/solution.py
+++ b/solution.py
@@ -53,27 +53,21 @@
 
 
 def times_cols(tile, x, out):
-    def rows(a, carry):
-        start = pl.multiple_of(a * 128, 128)
-        acc = tile[0, pl.ds(start, 128), :] * x[0:1, :]
+    for a in range(8):
+        rows = pl.ds(a * 128, 128)
+        acc = tile[0, rows, :] * x[0:1, :]
         for b in range(1, 8):
-            acc += tile[b, pl.ds(start, 128), :] * x[b : b + 1, :]
-        out[pl.ds(a, 1), :] = jnp.sum(acc.T, axis=0, keepdims=True)
-        return carry
-
-    lax.fori_loop(0, 8, rows, 0)
+            acc += tile[b, rows, :] * x[b : b + 1, :]
+        out[a : a + 1, :] = jnp.sum(acc.T, axis=0, keepdims=True)
 
 
 def times_rows(tile, x_ref, out):
-    def rows(a, sums):
-        start = pl.multiple_of(a * 128, 128)
-        x = jnp.broadcast_to(x_ref[pl.ds(a, 1), :], (128, 128)).T
-        return tuple(
-            s + jnp.sum((tile[b, pl.ds(start, 128), :] * x).reshape(16, 8, 128), axis=0)
-            for b, s in enumerate(sums)
-        )
-
-    sums = lax.fori_loop(0, 8, rows, (jnp.zeros((8, 128), F32),) * 8)
+    sums = [jnp.zeros((8, 128), F32)] * 8
+    for a in range(8):
+        x = jnp.broadcast_to(x_ref[a : a + 1, :], (128, 128)).T
+        for b in range(8):
+            line = tile[b, pl.ds(a * 128, 128), :] * x
+            sums[b] += jnp.sum(line.reshape(16, 8, 128), axis=0)
     for b in range(8):
         out[b : b + 1, :] = jnp.sum(sums[b], axis=0, keepdims=True)
 
@@ -127,12 +121,8 @@
         lines[pl.ds(128 * a, 128), :] = jnp.broadcast_to(x_ref[a : a + 1, :], (128, 128)).T
     for b in range(8):
         copies[b].wait()
-
-        def rows(a, acc):
-            at = pl.ds(pl.multiple_of(a * 128, 128), 128)
-            return acc + jnp.sum((held[b, at, :] * lines[at, :]).reshape(16, 8, 128), axis=0)
-
-        line = jnp.sum(lax.fori_loop(0, 8, rows, jnp.zeros((8, 128), F32)), axis=0, keepdims=True)
+        line = jnp.sum((held[b] * lines[...]).reshape(128, 8, 128), axis=0)
+        line = jnp.sum(line, axis=0, keepdims=True)
         for q in range(PEERS):
             payload[q, 0, b : b + 1, :] = line
     for q in range(PEERS):
@@ -140,12 +130,18 @@
         payload[q, 2] = panel[0, 1]
 
 
-def finish_image(j, got, us, ws, coeffs):
-    y = got
+def rayleigh(j, product, u, coeffs):
+    gamma = dot(u, product)
     for k in range(j):
-        y = y - us[k][...] * coeffs[k] - ws[k][...] * coeffs[K + k]
-    gamma = dot(us[j][...], y)
-    return y, gamma, 2.0 * y - 2.0 * gamma * us[j][...]
+        gamma = gamma - 2.0 * coeffs[k] * coeffs[K + k]
+    return gamma
+
+
+def image(j, product, us, ws, coeffs, gamma):
+    y = product
+    for k in range(j):
+        y = y - us[k] * coeffs[k] - ws[k] * coeffs[K + k]
+    return y, 2.0 * y - 2.0 * gamma * us[j]
 
 
 def step_kernel(j, *refs):
@@ -173,7 +169,11 @@
     next_own = spare[j - 1, 2] if j % 2 else late[mine, at + 1]
     x = column
     if j > 0:
-        y, gamma, w = finish_image(j - 1, got[:, 1], us, ws, coeffs_before)
+        before = got[:, 1]
+        gamma = rayleigh(j - 1, before, us[j - 1][...], coeffs_before)
+        y, w = image(
+            j - 1, before, [v[...] for v in us], [v[...] for v in ws], coeffs_before, gamma
+        )
         w_out[...] = w
         ws = ws + [w_out]
         bend = head(us[j - 1][0], j)
@@ -183,17 +183,17 @@
             x = x - us[k][...] * head(ws[k][0], j) - ws[k][...] * head(us[k][0], j)
     x = jnp.where(ids > j, x, 0.0)
     norm = jnp.sqrt(dot(x, x))
-    denom = jnp.sqrt(2.0 * norm * (norm + head(x[0], j + 1)) + EPS)
-    u = (x + jnp.where(ids == j + 1, norm, 0.0)) / denom
+    scale = 1.0 / jnp.sqrt(2.0 * norm * (norm + head(x[0], j + 1)) + EPS)
+    u = (x + jnp.where(ids == j + 1, norm, 0.0)) * scale
     u_out[...] = u
-    image = (summed + norm * next_own) / denom
+    product_own = (summed + norm * next_own) * scale
     for k in range(j):
-        coeffs[k] = dot(ws[k][...], u)
-        coeffs[K + k] = dot(us[k][...], u)
+        for n, v in ((k, ws[k]), (K + k, us[k])):
+            coeffs[n] = (dot(v[...], x) + norm * head(v[0], j + 1)) * scale
     if j == K - 1:
-        send(payload, [image])
+        send(payload, [product_own])
         return
-    y_own = image
+    y_own = product_own
     x_own = next_own
     for k in range(j):
         u_own, w_own = us[k][mine], ws[k][mine]
@@ -204,10 +204,10 @@
     x_ref[...] = x_own
     if j % 2:
         times_rows(tile, x_ref, product)
-        send(payload, [product[...], image, spare[j - 1, 2], spare[j, 2]])
+        send(payload, [product[...], product_own, spare[j - 1, 2], spare[j, 2]])
     else:
         times_cols(tile, x_own, product)
-        send(payload, [product[...], image] + ([spare[0, 2]] if j == 0 else []))
+        send(payload, [product[...], product_own] + ([spare[0, 2]] if j == 0 else []))
 
 
 def thirds(value):
@@ -218,32 +218,37 @@
 
 
 def last_kernel(place, got, coeffs, *refs):
-    us, ws = refs[:K], list(refs[K : 2 * K - 1])
-    tile, updated, images, w_ref, right, result, sem = refs[2 * K - 1 :]
-    row, col = place[0], place[1]
-    _, _, w = finish_image(K - 1, got[:, 0], us, ws, coeffs)
-    w_ref[...] = w
-    ws = ws + [w_ref]
+    us, ws = refs[:K], refs[K : 2 * K - 1]
+    tile, updated, images, right, result, sem = refs[2 * K - 1 :]
+    gamma = rayleigh(K - 1, got[:, 0], us[K - 1][...], coeffs)
+    shares = []
+    for mine in (place[0], place[1]):
+        u_own, w_own = [v[mine] for v in us], [v[mine] for v in ws]
+        _, w = image(K - 1, got[mine, 0], u_own, w_own, coeffs, gamma)
+        shares.append((u_own, [*w_own, w]))
+    (u_row, w_row), (u_col, w_col) = shares
     for k in range(K):
-        images[k] = ws[k][row]
+        images[k] = w_row[k]
     pad = jnp.zeros((32, 128), F32)
     for b in range(8):
-        high, middle, low = thirds(jnp.concatenate([v[col, b : b + 1] for v in [*ws, *us]], axis=0))
+        high, middle, low = thirds(jnp.concatenate([v[b : b + 1] for v in [*w_col, *u_col]], axis=0))
         right[:, 128 * b : 128 * (b + 1)] = jnp.concatenate(
             [high, middle, high, low, middle, high, pad], axis=0
         ).astype(jnp.bfloat16)
     copies = []
     for a in range(8):
-        high, middle, low = thirds(jnp.concatenate([v[row, a : a + 1] for v in [*us, *ws]], axis=0))
+        high, middle, low = thirds(jnp.concatenate([v[a : a + 1] for v in [*u_row, *w_row]], axis=0))
         left = jnp.concatenate([high, high, middle, high, middle, low, pad], axis=0).T.astype(jnp.bfloat16)
         change = jnp.dot(left, right[...], preferred_element_type=F32)
         for b in range(8):
-            rows = pl.ds(128 * a, 128)
-            result[b, rows, :] = tile[b, rows, :] - change[:, 128 * b : 128 * (b + 1)]
-            copies.append(
-                pltpu.make_async_copy(result.at[b, rows, :], updated.at[rows, b, :], sem.at[8 * a + b])
+            block = tile[b, pl.ds(128 * a, 128), :] - change[:, 128 * b : 128 * (b + 1)]
+            result[pl.ds(1024 * a + b, 128, stride=8), :] = block
+        copies.append(
+            pltpu.make_async_copy(
+                result.at[pl.ds(1024 * a, 1024), :], updated.at[pl.ds(1024 * a, 1024), :], sem.at[a]
             )
-            copies[-1].start()
+        )
+        copies[-1].start()
     for copy in copies:
         copy.wait()
 
@@ -350,14 +355,13 @@
     got = exchange(payload, "row")
     updated, images = pl.pallas_call(
         last_kernel,
-        out_shape=(jax.ShapeDtypeStruct((1024, 8, 128), F32), jax.ShapeDtypeStruct((K, 8, 128), F32)),
+        out_shape=(jax.ShapeDtypeStruct((8192, 128), F32), jax.ShapeDtypeStruct((K, 8, 128), F32)),
         in_specs=[smem()] + [vmem()] * (2 * K + 2),
         out_specs=[hbm, vmem()],
         scratch_shapes=[
-            pltpu.VMEM((PEERS, 8, 128), F32),
             pltpu.VMEM((128, 1024), jnp.bfloat16),
-            pltpu.VMEM((8, 1024, 128), F32),
-            pltpu.SemaphoreType.DMA((64,)),
+            pltpu.VMEM((8192, 128), F32),
+            pltpu.SemaphoreType.DMA((8,)),
         ],
         compiler_params=params(),
         cost_estimate=cost(2**25, 2**23),

time: 154 us -> 149 us (0.968)
  Pallas kernels: 28.4 us -> 23.5 us
    pallas_call x8, Pallas kernels: 14.4 us -> 10.3 us  [body(): pl.pallas_call(functools.partial(step_kernel, j), out_shape=outs, in_spec...]
where the time goes in v3:
time: 149 us
  blocking collectives  109 us (73%)
  Pallas kernels  23.5 us (16%)
  starting transfers between devices  9.98 us (7%)
  waiting for transfers between devices  5.59 us (4%)
    all_to_all x9, blocking collectives, exchange(): lax.all_to_all(payload, axis, split_axis=0, concat_axis=0, tiled=True)  109 us
    pallas_call x8, Pallas kernels, body(): pl.pallas_call(functools.partial(step_kernel, j), out_shape=outs, in_spec...  10.3 us
    all_to_all x1, starting transfers between devices, exchange(): lax.all_to_all(payload, axis, split_axis=0, concat_axis=0, tiled=True)  9.98 us
    all_to_all x1, waiting for transfers between devices, exchange(): lax.all_to_all(payload, axis, split_axis=0, concat_axis=0, tiled=True)  5.59 us
    pallas_call x1, Pallas kernels, body(): pl.pallas_call(load_kernel, out_shape=(jax.ShapeDtypeStruct((40, 1024, 12...  4.52 us
    pallas_call x1, Pallas kernels, body(): pl.pallas_call(last_kernel, out_shape=(jax.ShapeDtypeStruct((8192, 128),...  3.66 us
  transfers between devices with their start and end apart: 1, of which 1 were waited for; matrix products, arithmetic and copies ran while one was open for 0% of the time, Pallas kernels for 3%

profile of v3, /device:TPU:1, one launch (start us, length us, event | category | flops | bytes accessed | tf_op | source)
XLA Modules:
  0.0 149.0 jit_solution(1743043233678197402)
XLA Ops:
  0.6 2.2 %shard_map.30 = f32[16,3,8,128]{3,2,1,0:T(8,128)} custom-call(f32[1024,8,128]{2,1,0:T(8,128)} %bitcast.9), custom_call_target="tpu_custom_call" | custom-call | flops 1048576 | bytes 1048576 | tf_op jit(solution)/shard_map/pallas_call | solution.py:273
  2.8 10.0 %all-to-all-start = ((f32[16,3,8,128]{3,2,1,0:T(8,128)}), f32[16,3,8,128]{3,2,1,0:T(8,128)S(1)}, u32[]{:S(2)}, u32[]{:S(2)}) async-start(f32[16,3,8,128]{3,2,1,0:T(8,128)} %shard_map.30), calls=%async_computation | async-start | bytes 393216 | tf_op jit(solution)/shard_map/all_to_all | solution.py:265
  12.8 4.5 %shard_map.31 = (f32[40,1024,128]{2,1,0:T(8,128)}, f32[8,1024,128]{2,1,0:T(8,128)}) custom-call(f32[1024,8,128]{2,1,0:T(8,128)} %bitcast.10), custom_call_target="tpu_custom_call" | custom-call | flops 2097152 | bytes 8388608 | tf_op jit(solution)/shard_map/pallas_call | solution.py:287
  17.3 0.1 pad_add_fusion.place.refs_0_
  17.4 5.6 %all-to-all-done.panel.refs_2_ = f32[16,3,8,128]{3,2,1,0:T(8,128)S(1)} async-done(((f32[16,3,8,128]{3,2,1,0:T(8,128)}), f32[16,3,8,128]{3,2,1,0:T(8,128)S(1)}, u32[]{:S(2)}, u32[]{:S(2)}) %all-to-all-start) | async-done | bytes 196640 | tf_op jit(solution)/shard_map/all_to_all | solution.py:265
  23.0 2.9 %shard_map.32 = (f32[16,3,8,128]{3,2,1,0:T(8,128)S(1)}, f32[8,1024,128]{2,1,0:T(8,128)S(1)}) custom-call(s32[2]{0:T(128)S(1)} %pad_add_fusion.place.refs_0_, f32[16,3,8,128]{3,2,1,0:T(8,128)S(1)} %all-to-all-done.panel.refs_2_, f32[40,1024,128]{2,1,0:T(8,128)} %get-tuple-element.39.tile), custom_call_target="tpu_custom_call" | custom-call | flops 2097152 | bytes 4194304 | tf_op jit(solution)/shard_map/pallas_call | solution.py:303
  25.9 14.5 %all_to_all.50.refs_1_.refs_2_ = f32[16,3,8,128]{3,2,1,0:T(8,128)S(1)} all-to-all(f32[16,3,8,128]{3,2,1,0:T(8,128)S(1)} %get-tuple-element.40), channel_id=1, replica_groups=mesh['row'=16,'col'=16] {'row'}, dimensions={0} | all-to-all | bytes 393216 | tf_op jit(solution)/shard_map/all_to_all | solution.py:265
  40.5 1.1 step_0.1
  41.6 13.3 %all_to_all.51.refs_1_.refs_2_ = f32[16,3,8,128]{3,2,1,0:T(8,128)S(1)} all-to-all(f32[16,3,8,128]{3,2,1,0:T(8,128)S(1)} %get-tuple-element.42), channel_id=1, replica_groups=mesh['row'=16,'col'=16] {'col'}, dimensions={0} | all-to-all | bytes 393216 | tf_op jit(solution)/shard_map/all_to_all | solution.py:265
  54.9 1.4 step_1.1
  56.2 11.3 %all_to_all.52.refs_1_.refs_3_ = f32[16,4,8,128]{3,2,1,0:T(8,128)S(1)} all-to-all(f32[16,4,8,128]{3,2,1,0:T(8,128)S(1)} %get-tuple-element.45), channel_id=1, replica_groups=mesh['row'=16,'col'=16] {'row'}, dimensions={0} | all-to-all | bytes 524288 | tf_op jit(solution)/shard_map/all_to_all | solution.py:265
  67.6 1.3 step_2.1
  68.9 12.6 %all_to_all.53.refs_1_ = f32[16,2,8,128]{3,2,1,0:T(8,128)S(1)} all-to-all(f32[16,2,8,128]{3,2,1,0:T(8,128)S(1)} %get-tuple-element.49), channel_id=1, replica_groups=mesh['row'=16,'col'=16] {'col'}, dimensions={0} | all-to-all | bytes 262144 | tf_op jit(solution)/shard_map/all_to_all | solution.py:265
  81.5 1.4 step_3.1
  82.8 11.2 %all_to_all.54.refs_1_.refs_3_ = f32[16,4,8,128]{3,2,1,0:T(8,128)S(1)} all-to-all(f32[16,4,8,128]{3,2,1,0:T(8,128)S(1)} %get-tuple-element.53), channel_id=1, replica_groups=mesh['row'=16,'col'=16] {'row'}, dimensions={0} | all-to-all | bytes 524288 | tf_op jit(solution)/shard_map/all_to_all | solution.py:265
  94.0 1.4 step_4.1
  95.3 12.7 %all_to_all.55.refs_1_ = f32[16,2,8,128]{3,2,1,0:T(8,128)S(1)} all-to-all(f32[16,2,8,128]{3,2,1,0:T(8,128)S(1)} %get-tuple-element.57), channel_id=1, replica_groups=mesh['row'=16,'col'=16] {'col'}, dimensions={0} | all-to-all | bytes 262144 | tf_op jit(solution)/shard_map/all_to_all | solution.py:265
  108.0 1.4 step_5.1
  109.4 0.0 copy-start
  109.4 11.4 %all_to_all.56.refs_1_.refs_3_ = f32[16,4,8,128]{3,2,1,0:T(8,128)S(1)} all-to-all(f32[16,4,8,128]{3,2,1,0:T(8,128)S(1)} %get-tuple-element.61), channel_id=1, replica_groups=mesh['row'=16,'col'=16] {'row'}, dimensions={0} | all-to-all | bytes 524288 | tf_op jit(solution)/shard_map/all_to_all | solution.py:265
  120.9 1.4 step_6.1
  122.2 12.7 %all_to_all.57.refs_1_ = f32[16,2,8,128]{3,2,1,0:T(8,128)S(1)} all-to-all(f32[16,2,8,128]{3,2,1,0:T(8,128)S(1)} %get-tuple-element.65), channel_id=1, replica_groups=mesh['row'=16,'col'=16] {'col'}, dimensions={0} | all-to-all | bytes 262144 | tf_op jit(solution)/shard_map/all_to_all | solution.py:265
  134.9 1.0 step_7.1
  135.9 9.4 %all_to_all.58.got = f32[16,1,8,128]{3,2,1,0:T(8,128)S(1)} all-to-all(f32[16,1,8,128]{3,2,1,0:T(8,128)S(1)} %get-tuple-element.69), channel_id=1, replica_groups=mesh['row'=16,'col'=16] {'row'}, dimensions={0} | all-to-all | bytes 131072 | tf_op jit(solution)/shard_map/all_to_all | solution.py:265
  145.3 0.0 copy-done
  145.3 3.7 %shard_map.33 = (f32[8192,128]{1,0:T(8,128)}, f32[8,8,128]{2,1,0:T(8,128)}) custom-call(s32[2]{0:T(128)S(1)} %pad_add_fusion.place.refs_0_, f32[16,1,8,128]{3,2,1,0:T(8,128)S(1)} %all_to_all.58.got, f32[16,8,128]{2,1,0:T(8,128)S(1)} %get-tuple-element.70.coeffs, f32[16,8,128]{2,1,0:T(8,128)S(1)} %get-tuple-element.43.refs_4_.refs_3_.refs_5_.refs_0_, ...), custom_call_target="tpu_custom_call" | custom-call | flops 33554432 | bytes 8388608 | tf_op jit(solution)/shard_map/pallas_call | solution.py:356
Async XLA Ops:
  2.8 20.2 %all-to-all-start = ((f32[16,3,8,128]{3,2,1,0:T(8,128)}), f32[16,3,8,128]{3,2,1,0:T(8,128)S(1)}, u32[]{:S(2)}, u32[]{:S(2)}) async-start(f32[16,3,8,128]{3,2,1,0:T(8,128)} %shard_map.30), calls=%async_computation | async-start | bytes 393216 | tf_op jit(solution)/shard_map/all_to_all | solution.py:265
  109.4 35.9 %copy-start = (f32[8,1024,128]{2,1,0:T(8,128)S(1)}, f32[8,1024,128]{2,1,0:T(8,128)}, u32[]{:S(2)}) copy-start(f32[8,1024,128]{2,1,0:T(8,128)} %get-tuple-element.73.refs_15_) | copy-start | bytes 12582916

commit v4 on v3

--- a/solution.py
+++ b/solution.py
@@ -79,13 +79,10 @@
 
 
 def panel_kernel(matrix, payload, corner, panel, sem):
-    copies = []
-    for a in range(8):
-        rows = pl.ds(128 * a, 128)
-        copies.append(pltpu.make_async_copy(matrix.at[rows, 0, :], corner.at[rows], sem.at[a]))
-        copies[-1].start()
-    for a in range(8):
-        copies[a].wait()
+    copy = pltpu.make_async_copy(matrix.at[:, 0, :], corner, sem)
+    copy.start()
+    copy.wait()
+    for a in range(8):
         lines = corner[pl.ds(128 * a, 128), :].T
         for k in range(K + 1):
             panel[k, a : a + 1, :] = lines[k : k + 1, :]
@@ -278,7 +275,7 @@
         scratch_shapes=[
             pltpu.VMEM((1024, 128), F32),
             pltpu.VMEM((K + 1, 8, 128), F32),
-            pltpu.SemaphoreType.DMA((8,)),
+            pltpu.SemaphoreType.DMA,
         ],
         compiler_params=params(WIDE),
         cost_estimate=cost(2**20, 2**20),

time: 149 us -> 149 us (level)
  no operation moved by 1% of the time
where the time goes in v4:
time: 149 us
  blocking collectives  109 us (73%)
  Pallas kernels  23.3 us (16%)
  starting transfers between devices  9.98 us (7%)
  waiting for transfers between devices  5.59 us (4%)
    all_to_all x9, blocking collectives, exchange(): lax.all_to_all(payload, axis, split_axis=0, concat_axis=0, tiled=True)  109 us
    pallas_call x8, Pallas kernels, body(): pl.pallas_call(functools.partial(step_kernel, j), out_shape=outs, in_spec...  10.3 us
    all_to_all x1, starting transfers between devices, exchange(): lax.all_to_all(payload, axis, split_axis=0, concat_axis=0, tiled=True)  9.98 us
    all_to_all x1, waiting for transfers between devices, exchange(): lax.all_to_all(payload, axis, split_axis=0, concat_axis=0, tiled=True)  5.59 us
    pallas_call x1, Pallas kernels, body(): pl.pallas_call(load_kernel, out_shape=(jax.ShapeDtypeStruct((40, 1024, 12...  4.52 us
    pallas_call x1, Pallas kernels, body(): pl.pallas_call(last_kernel, out_shape=(jax.ShapeDtypeStruct((8192, 128),...  3.66 us
  transfers between devices with their start and end apart: 1, of which 1 were waited for; matrix products, arithmetic and copies ran while one was open for 0% of the time, Pallas kernels for 3%

profile of v4, /device:TPU:1, one launch (start us, length us, event | category | flops | bytes accessed | tf_op | source)
XLA Modules:
  0.0 148.7 jit_solution(2549010635461350874)
XLA Ops:
  0.6 1.9 %shard_map.30 = f32[16,3,8,128]{3,2,1,0:T(8,128)} custom-call(f32[1024,8,128]{2,1,0:T(8,128)} %bitcast.9), custom_call_target="tpu_custom_call" | custom-call | flops 1048576 | bytes 1048576 | tf_op jit(solution)/shard_map/pallas_call | solution.py:270
  2.5 10.0 %all-to-all-start = ((f32[16,3,8,128]{3,2,1,0:T(8,128)}), f32[16,3,8,128]{3,2,1,0:T(8,128)S(1)}, u32[]{:S(2)}, u32[]{:S(2)}) async-start(f32[16,3,8,128]{3,2,1,0:T(8,128)} %shard_map.30), calls=%async_computation | async-start | bytes 393216 | tf_op jit(solution)/shard_map/all_to_all | solution.py:262
  12.5 4.5 %shard_map.31 = (f32[40,1024,128]{2,1,0:T(8,128)}, f32[8,1024,128]{2,1,0:T(8,128)}) custom-call(f32[1024,8,128]{2,1,0:T(8,128)} %bitcast.10), custom_call_target="tpu_custom_call" | custom-call | flops 2097152 | bytes 8388608 | tf_op jit(solution)/shard_map/pallas_call | solution.py:284
  17.1 0.1 pad_add_fusion.place.refs_0_
  17.1 5.6 %all-to-all-done.panel.refs_2_ = f32[16,3,8,128]{3,2,1,0:T(8,128)S(1)} async-done(((f32[16,3,8,128]{3,2,1,0:T(8,128)}), f32[16,3,8,128]{3,2,1,0:T(8,128)S(1)}, u32[]{:S(2)}, u32[]{:S(2)}) %all-to-all-start) | async-done | bytes 196640 | tf_op jit(solution)/shard_map/all_to_all | solution.py:262
  22.7 2.9 %shard_map.32 = (f32[16,3,8,128]{3,2,1,0:T(8,128)S(1)}, f32[8,1024,128]{2,1,0:T(8,128)S(1)}) custom-call(s32[2]{0:T(128)S(1)} %pad_add_fusion.place.refs_0_, f32[16,3,8,128]{3,2,1,0:T(8,128)S(1)} %all-to-all-done.panel.refs_2_, f32[40,1024,128]{2,1,0:T(8,128)} %get-tuple-element.39.tile), custom_call_target="tpu_custom_call" | custom-call | flops 2097152 | bytes 4194304 | tf_op jit(solution)/shard_map/pallas_call | solution.py:300
  25.6 14.5 %all_to_all.50.refs_1_.refs_2_ = f32[16,3,8,128]{3,2,1,0:T(8,128)S(1)} all-to-all(f32[16,3,8,128]{3,2,1,0:T(8,128)S(1)} %get-tuple-element.40), channel_id=1, replica_groups=mesh['row'=16,'col'=16] {'row'}, dimensions={0} | all-to-all | bytes 393216 | tf_op jit(solution)/shard_map/all_to_all | solution.py:262
  40.2 1.1 step_0.1
  41.3 13.3 %all_to_all.51.refs_1_.refs_2_ = f32[16,3,8,128]{3,2,1,0:T(8,128)S(1)} all-to-all(f32[16,3,8,128]{3,2,1,0:T(8,128)S(1)} %get-tuple-element.42), channel_id=1, replica_groups=mesh['row'=16,'col'=16] {'col'}, dimensions={0} | all-to-all | bytes 393216 | tf_op jit(solution)/shard_map/all_to_all | solution.py:262
  54.6 1.4 step_1.1
  56.0 11.3 %all_to_all.52.refs_1_.refs_3_ = f32[16,4,8,128]{3,2,1,0:T(8,128)S(1)} all-to-all(f32[16,4,8,128]{3,2,1,0:T(8,128)S(1)} %get-tuple-element.45), channel_id=1, replica_groups=mesh['row'=16,'col'=16] {'row'}, dimensions={0} | all-to-all | bytes 524288 | tf_op jit(solution)/shard_map/all_to_all | solution.py:262
  67.3 1.3 step_2.1
  68.6 12.6 %all_to_all.53.refs_1_ = f32[16,2,8,128]{3,2,1,0:T(8,128)S(1)} all-to-all(f32[16,2,8,128]{3,2,1,0:T(8,128)S(1)} %get-tuple-element.49), channel_id=1, replica_groups=mesh['row'=16,'col'=16] {'col'}, dimensions={0} | all-to-all | bytes 262144 | tf_op jit(solution)/shard_map/all_to_all | solution.py:262
  81.2 1.4 step_3.1
  82.6 11.2 %all_to_all.54.refs_1_.refs_3_ = f32[16,4,8,128]{3,2,1,0:T(8,128)S(1)} all-to-all(f32[16,4,8,128]{3,2,1,0:T(8,128)S(1)} %get-tuple-element.53), channel_id=1, replica_groups=mesh['row'=16,'col'=16] {'row'}, dimensions={0} | all-to-all | bytes 524288 | tf_op jit(solution)/shard_map/all_to_all | solution.py:262
  93.7 1.4 step_4.1
  95.1 12.7 %all_to_all.55.refs_1_ = f32[16,2,8,128]{3,2,1,0:T(8,128)S(1)} all-to-all(f32[16,2,8,128]{3,2,1,0:T(8,128)S(1)} %get-tuple-element.57), channel_id=1, replica_groups=mesh['row'=16,'col'=16] {'col'}, dimensions={0} | all-to-all | bytes 262144 | tf_op jit(solution)/shard_map/all_to_all | solution.py:262
  107.8 1.4 step_5.1
  109.1 0.0 copy-start
  109.2 11.4 %all_to_all.56.refs_1_.refs_3_ = f32[16,4,8,128]{3,2,1,0:T(8,128)S(1)} all-to-all(f32[16,4,8,128]{3,2,1,0:T(8,128)S(1)} %get-tuple-element.61), channel_id=1, replica_groups=mesh['row'=16,'col'=16] {'row'}, dimensions={0} | all-to-all | bytes 524288 | tf_op jit(solution)/shard_map/all_to_all | solution.py:262
  120.6 1.4 step_6.1
  122.0 12.7 %all_to_all.57.refs_1_ = f32[16,2,8,128]{3,2,1,0:T(8,128)S(1)} all-to-all(f32[16,2,8,128]{3,2,1,0:T(8,128)S(1)} %get-tuple-element.65), channel_id=1, replica_groups=mesh['row'=16,'col'=16] {'col'}, dimensions={0} | all-to-all | bytes 262144 | tf_op jit(solution)/shard_map/all_to_all | solution.py:262
  134.6 1.0 step_7.1
  135.6 9.4 %all_to_all.58.got = f32[16,1,8,128]{3,2,1,0:T(8,128)S(1)} all-to-all(f32[16,1,8,128]{3,2,1,0:T(8,128)S(1)} %get-tuple-element.69), channel_id=1, replica_groups=mesh['row'=16,'col'=16] {'row'}, dimensions={0} | all-to-all | bytes 131072 | tf_op jit(solution)/shard_map/all_to_all | solution.py:262
  145.0 0.0 copy-done
  145.0 3.7 %shard_map.33 = (f32[8192,128]{1,0:T(8,128)}, f32[8,8,128]{2,1,0:T(8,128)}) custom-call(s32[2]{0:T(128)S(1)} %pad_add_fusion.place.refs_0_, f32[16,1,8,128]{3,2,1,0:T(8,128)S(1)} %all_to_all.58.got, f32[16,8,128]{2,1,0:T(8,128)S(1)} %get-tuple-element.70.coeffs, f32[16,8,128]{2,1,0:T(8,128)S(1)} %get-tuple-element.43.refs_4_.refs_3_.refs_5_.refs_0_, ...), custom_call_target="tpu_custom_call" | custom-call | flops 33554432 | bytes 8388608 | tf_op jit(solution)/shard_map/pallas_call | solution.py:353
Async XLA Ops:
  2.5 20.2 %all-to-all-start = ((f32[16,3,8,128]{3,2,1,0:T(8,128)}), f32[16,3,8,128]{3,2,1,0:T(8,128)S(1)}, u32[]{:S(2)}, u32[]{:S(2)}) async-start(f32[16,3,8,128]{3,2,1,0:T(8,128)} %shard_map.30), calls=%async_computation | async-start | bytes 393216 | tf_op jit(solution)/shard_map/all_to_all | solution.py:262
  109.1 35.9 %copy-start = (f32[8,1024,128]{2,1,0:T(8,128)S(1)}, f32[8,1024,128]{2,1,0:T(8,128)}, u32[]{:S(2)}) copy-start(f32[8,1024,128]{2,1,0:T(8,128)} %get-tuple-element.73.refs_15_) | copy-start | bytes 12582916
